TPU v7x, 256 devices: a whole 4x4x8 slice. The times are simulated.
256 devices in a mesh: trow: 16 (over x, y), tcol: 8 (over z), rep: 2 (over core).
Axes of the slice: x: 4, y: 4, z: 8, core: 2. Of those that a mesh axis runs over, the one named last changes fastest.
Arguments:
- users: float32 [131072, 128], P(('trow', 'tcol'))
- items: float32 [65536, 128], P(('tcol', 'trow'))
- ratings: bfloat16 [16, 8, 2, 64, 128, 128], P('trow', 'tcol', 'rep'), may hold values from -6 to 6
- row_mask: int32 [16, 8, 2, 64, 128], P('trow', 'tcol', 'rep'), may hold values 0 or 1
- col_mask: int32 [16, 8, 2, 64, 128], P('trow', 'tcol', 'rep'), may hold values 0 or 1
- row_slots: int32 [16, 8, 2, 64], P('trow', 'tcol', 'rep'), may hold values from 0 to 31, as said below
- col_slots: int32 [16, 8, 2, 64], P('trow', 'tcol', 'rep'), may hold values from 0 to 31, as said below
- send_users: int32 [16, 8, 2, 8, 4], P('trow', 'tcol', 'rep'), may hold values from 0 to 7, as said below
- send_items: int32 [16, 8, 2, 16, 2], P('trow', 'tcol', 'rep'), may hold values from 0 to 3, as said below
Outputs:
- users_out: float32 [131072, 128], P(('trow', 'tcol'))
- items_out: float32 [65536, 128], P(('tcol', 'trow'))
Inputs may be any that keep to these rules, and one draw needn't show every extreme that they name: `send_users`: distinct within each row of the last dimension. `send_items`: distinct within each row of the last dimension. `row_slots`: every slot is named by some tile of each device. `col_slots`: every slot is named by some tile of each device.
All inputs are finite; a program needn't handle non-finite values. No bound on the sum of `row_mask` or of `col_mask` on one device may be relied on, other than what follows from the above.
Results may differ from a plain program's by a relative error of at most 0.02.
Values may be sent and summed in bfloat16 or wider, within the bound.
A program may use at most 64 MiB of HBM per device.

v0:
```python
import jax
import jax.numpy as jnp
from jax import lax
from jax.sharding import PartitionSpec as P

ITERS = 2


def precondition(gradient, gramian):
    factor = jnp.linalg.cholesky(gramian)
    return jax.scipy.linalg.cho_solve((factor, True), gradient.T).T


def pool_sum(index_list, terms, pool_count):
    onehot = (
        lax.broadcasted_iota(jnp.int32, (pool_count, index_list.shape[0]), 0) == index_list[None, :]
    ).astype(jnp.bfloat16)
    flat = terms.reshape(terms.shape[0], -1)
    upper = flat.astype(jnp.bfloat16)
    lower = (flat - upper.astype(jnp.float32)).astype(jnp.bfloat16)
    return jnp.dot(onehot, upper, preferred_element_type=jnp.float32) + jnp.dot(
        onehot, lower, preferred_element_type=jnp.float32
    )


def on_device(
    users, items, ratings, row_mask, col_mask, row_slots, col_slots, send_users, send_items
):
    n_trow = lax.axis_size("trow")
    n_tcol = lax.axis_size("tcol")
    n_rep = lax.axis_size("rep")
    tile_size = ratings.shape[-1]
    rank_width = users.shape[1]
    tile_count = ratings.shape[3]
    own_users = users.shape[0] // tile_size
    own_items = items.shape[0] // tile_size
    user_cap = send_users.shape[-1]
    item_cap = send_items.shape[-1]
    ratings_local = ratings.reshape(tile_count, tile_size, tile_size)
    weights = (
        row_mask.reshape(tile_count, tile_size)[:, :, None]
        * col_mask.reshape(tile_count, tile_size)[:, None, :]
    ).astype(jnp.float32)
    row_slot_list = row_slots.reshape(-1)
    col_slot_list = col_slots.reshape(-1)
    user_sends = send_users.reshape(n_tcol, -1)
    item_sends = send_items.reshape(n_trow, -1)
    user_received = lax.all_to_all(
        user_sends, "tcol", split_axis=0, concat_axis=0, tiled=True
    ).reshape(-1)
    item_received = lax.all_to_all(
        item_sends, "trow", split_axis=0, concat_axis=0, tiled=True
    ).reshape(-1)
    row_list = row_slot_list // user_cap * own_users + user_received[row_slot_list]
    col_list = col_slot_list // item_cap * own_items + item_received[col_slot_list]
    all_users = own_users * tile_size * n_trow * n_tcol
    all_items = own_items * tile_size * n_trow * n_tcol
    user_coef = 2.0 * all_items * own_users / (tile_size * tile_count * n_rep)
    item_coef = 2.0 * all_users * own_items / (tile_size * tile_count * n_rep)
    for iteration in range(ITERS):
        gram_users, gram_items = lax.psum(
            (
                jnp.dot(
                    users.T,
                    users,
                    precision=lax.Precision.HIGHEST,
                    preferred_element_type=jnp.float32,
                ),
                jnp.dot(
                    items.T,
                    items,
                    precision=lax.Precision.HIGHEST,
                    preferred_element_type=jnp.float32,
                ),
            ),
            ("trow", "tcol"),
        )
        user_half = users.astype(jnp.bfloat16).reshape(own_users, tile_size, rank_width)
        item_half = items.astype(jnp.bfloat16).reshape(own_items, tile_size, rank_width)
        user_pool = lax.all_gather(user_half, "tcol", axis=0, tiled=True)
        item_pool = lax.all_gather(item_half, "trow", axis=0, tiled=True)
        x_tiles = user_pool[row_list]
        y_tiles = item_pool[col_list]
        predicted = jnp.einsum("tar,tbr->tab", x_tiles, y_tiles, preferred_element_type=jnp.float32)
        errors = (weights * (predicted - ratings_local.astype(jnp.float32))).astype(jnp.bfloat16)
        user_terms = jnp.einsum("tab,tbr->tar", errors, y_tiles, preferred_element_type=jnp.float32)
        item_terms = jnp.einsum("tab,tar->tbr", errors, x_tiles, preferred_element_type=jnp.float32)
        user_pooled = pool_sum(row_list, user_terms, user_pool.shape[0])
        item_pooled = pool_sum(col_list, item_terms, item_pool.shape[0])
        user_grad = lax.psum_scatter(user_pooled, "tcol", scatter_dimension=0, tiled=True)
        item_grad = lax.psum_scatter(item_pooled, "trow", scatter_dimension=0, tiled=True)
        user_grad, item_grad = lax.psum((user_grad, item_grad), "rep")
        new_users = users - user_coef * precondition(user_grad.reshape(-1, rank_width), gram_items)
        new_items = items - item_coef * precondition(item_grad.reshape(-1, rank_width), gram_users)
        users, items = (new_users, new_items)
    return (users, items)


def solution(mesh):
    return jax.shard_map(
        on_device,
        mesh=mesh,
        in_specs=(
            P(("trow", "tcol"), None),
            P(("tcol", "trow"), None),
            P("trow", "tcol", "rep", None, None, None),
            P("trow", "tcol", "rep", None, None),
            P("trow", "tcol", "rep", None, None),
            P("trow", "tcol", "rep", None),
            P("trow", "tcol", "rep", None),
            P("trow", "tcol", "rep", None, None),
            P("trow", "tcol", "rep", None, None),
        ),
        out_specs=(P(("trow", "tcol"), None), P(("tcol", "trow"), None)),
        check_vma=False,
    )
```

profile of v0, /device:TPU:1, one launch (start us, length us, event | category | flops | bytes accessed | tf_op | source)
XLA Modules:
  0.0 1075.5 jit_solution(2654260133140196737)
XLA Ops:
  12.1 7.6 all-to-all-start.1
  22.3 3.7 all-to-all-done.1
  26.1 8.2 all-to-all-start
  36.4 4.4 all-to-all-done
  42.3 9.4 all-gather.5.cloned.1.call-done
  51.7 3.7 gather_fusion.1
  55.4 50.8 %all-gather.7.cloned.1.call-done = bf16[64,128,128]{2,1,0:T(8,128)(2,1)} async-done(((bf16[4,128,128]{2,1,0:T(8,128)(2,1)}), bf16[64,128,128]{2,1,0:T(8,128)(2,1)}) %all-gather.7.cloned.1.call-update) | async-done | bytes 2097168 | tf_op jit(solution)/shard_map/all_gather | solution.py:81
  108.9 4.1 fusion.1
  117.2 4.9 convolution_add_fusion.2
  124.6 2.8 fusion.8
  127.4 4.9 convolution_add_fusion.3
  137.4 98.5 %all-reduce.13.cloned.1.call-done = f32[64,16384]{1,0:T(8,128)} async-done(((f32[64,16384]{1,0:T(8,128)}), f32[64,16384]{1,0:T(8,128)}) %all-reduce.13.cloned.1.call-update) | async-done | bytes 4194320
  237.9 55.8 %reduce-scatter.3.cloned.1.call-done = f32[8,16384]{1,0:T(8,128)} async-done(((f32[64,16384]{1,0:T(8,128)}), f32[8,16384]{1,0:T(8,128)}) %reduce-scatter.3.cloned.1.call-update) | async-done | bytes 524304 | tf_op jit(solution)/shard_map/reduce_scatter | solution.py:90
  296.1 209.1 %all-reduce.19.cloned.1.call-done = (f32[128,128]{0,1:T(8,128)}, f32[128,128]{0,1:T(8,128)}) async-done(((f32[128,128]{0,1:T(8,128)}, f32[128,128]{0,1:T(8,128)}), (f32[128,128]{0,1:T(8,128)}, f32[128,128]{0,1:T(8,128)})) %all-reduce.19.cloned.1.call-update) | async-done | bytes 131088 | tf_op jit(solution)/shard_map/psum | solution.py:61
  508.0 11.7 %cholesky.74 = f32[128,128]{1,0:T(8,128)S(1)} custom-call(f32[128,128]{1,0:T(8,128)S(1)} %get-tuple-element.24), custom_call_target="Cholesky" | custom-call | tf_op jit(solution)/shard_map/jit(cholesky)/cholesky | solution.py:10
  521.1 9.8 custom-call.14
  530.9 10.3 all-reduce.23.cloned.1.call-done
  545.1 11.7 %cholesky.85 = f32[128,128]{1,0:T(8,128)S(1)} custom-call(f32[128,128]{1,0:T(8,128)S(1)} %get-tuple-element.23), custom_call_target="Cholesky" | custom-call | tf_op jit(solution)/shard_map/jit(cholesky)/cholesky | solution.py:10
  558.1 9.8 custom-call.15
  572.0 10.9 %all-gather.9.cloned.1.call-done = bf16[64,128,128]{2,1,0:T(8,128)(2,1)} async-done(((bf16[8,128,128]{2,1,0:T(8,128)(2,1)}), bf16[64,128,128]{2,1,0:T(8,128)(2,1)}) %all-gather.9.cloned.1.call-update) | async-done | bytes 2097168 | tf_op jit(solution)/shard_map/all_gather | solution.py:80
  582.9 3.7 gather_fusion.4
  586.7 50.5 %all-gather.11.cloned.1.call-done = bf16[64,128,128]{2,1,0:T(8,128)(2,1)} async-done(((bf16[4,128,128]{2,1,0:T(8,128)(2,1)}), bf16[64,128,128]{2,1,0:T(8,128)(2,1)}) %all-gather.11.cloned.1.call-update) | async-done | bytes 2097168 | tf_op jit(solution)/shard_map/all_gather | solution.py:81
  639.7 4.1 fusion.3
  648.0 4.9 convolution_add_fusion
  658.1 4.9 convolution_add_fusion.1
  663.2 187.3 %all-reduce.17.cloned.1.call-done = (f32[128,128]{0,1:T(8,128)}, f32[128,128]{0,1:T(8,128)}) async-done(((f32[128,128]{0,1:T(8,128)}, f32[128,128]{0,1:T(8,128)}), (f32[128,128]{0,1:T(8,128)}, f32[128,128]{0,1:T(8,128)})) %all-reduce.17.cloned.1.call-update) | async-done | bytes 131088 | tf_op jit(solution)/shard_map/psum | solution.py:61
  852.4 11.7 %cholesky.96 = f32[128,128]{1,0:T(8,128)S(1)} custom-call(f32[128,128]{1,0:T(8,128)S(1)} %fusion.35), custom_call_target="Cholesky" | custom-call | tf_op jit(solution)/shard_map/jit(cholesky)/cholesky | solution.py:10
  864.8 104.5 %all-reduce.15.cloned.1.call-done = f32[64,16384]{1,0:T(8,128)} async-done(((f32[64,16384]{1,0:T(8,128)}), f32[64,16384]{1,0:T(8,128)}) %all-reduce.15.cloned.1.call-update) | async-done | bytes 4194320
  971.4 56.1 %reduce-scatter.5.cloned.1.call-done = f32[8,16384]{1,0:T(8,128)} async-done(((f32[64,16384]{1,0:T(8,128)}), f32[8,16384]{1,0:T(8,128)}) %reduce-scatter.5.cloned.1.call-update) | async-done | bytes 524304 | tf_op jit(solution)/shard_map/reduce_scatter | solution.py:90
  1030.1 9.8 custom-call.16
  1040.0 11.7 %cholesky.107 = f32[128,128]{1,0:T(8,128)S(1)} custom-call(f32[128,128]{1,0:T(8,128)S(1)} %fusion.31), custom_call_target="Cholesky" | custom-call | tf_op jit(solution)/shard_map/jit(cholesky)/cholesky | solution.py:10
  1053.2 10.0 custom-call.17
  (127 shorter events, 68.1 us)
Async XLA Ops:
  7.2 35.1 %copy-start.12 = (s32[1,1,1,64]{3,2,1,0:T(1,128)S(1)}, s32[1,1,1,64]{3,2,1,0:T(1,128)}, u32[]{:S(2)}) copy-start(s32[1,1,1,64]{3,2,1,0:T(1,128)} %param.19) | copy-start | bytes 772
  7.2 29.1 %copy-start.11 = (s32[1,1,1,64]{3,2,1,0:T(1,128)S(1)}, s32[1,1,1,64]{3,2,1,0:T(1,128)}, u32[]{:S(2)}) copy-start(s32[1,1,1,64]{3,2,1,0:T(1,128)} %param.20) | copy-start | bytes 772
  7.2 44.5 %all-gather.5.cloned.1.call-start = ((), (), s32[]{:S(2)}) async-start(), calls=%async_computation.4 | async-start | bytes 2359296 | tf_op jit(solution)/shard_map/all_gather | solution.py:80
  9.0 97.3 %all-gather.7.cloned.1.call-start = ((), (), s32[]{:S(2)}) async-start(), calls=%async_computation.5 | async-start | bytes 2228224 | tf_op jit(solution)/shard_map/all_gather | solution.py:81
  12.1 14.0 %all-to-all-start.1 = ((s32[16,1,2]{2,1,0:T(1,128)}), s32[16,1,2]{2,1,0:T(1,128)S(1)}, u32[]{:S(2)}, u32[]{:S(2)}) async-start(s32[16,1,2]{2,1,0:T(1,128)} %copy.48), calls=%async_computation.1 | async-start | bytes 16384 | tf_op jit(solution)/shard_map/all_to_all | solution.py:51
  26.1 14.7 %all-to-all-start = ((s32[8,1,4]{2,1,0:T(1,128)}), s32[8,1,4]{2,1,0:T(1,128)S(1)}, u32[]{:S(2)}, u32[]{:S(2)}) async-start(s32[8,1,4]{2,1,0:T(1,128)} %copy.47), calls=%async_computation | async-start | bytes 8192 | tf_op jit(solution)/shard_map/all_to_all | solution.py:48
  34.3 201.6 %all-reduce.13.cloned.1.call-start = ((), (), s32[]{:S(2)}) async-start(), calls=%async_computation.10 | async-start | bytes 8388608
  55.4 53.4 %copy-start.9 = (s32[1,1,1,64,128]{4,3,2,1,0:T(8,128)S(1)}, s32[1,1,1,64,128]{4,3,2,1,0:T(8,128)}, u32[]{:S(2)}) copy-start(s32[1,1,1,64,128]{4,3,2,1,0:T(8,128)} %param.18) | copy-start | bytes 98308
  55.4 53.4 %copy-start.10 = (s32[1,1,1,64,128]{4,3,2,1,0:T(8,128)S(1)}, s32[1,1,1,64,128]{4,3,2,1,0:T(8,128)}, u32[]{:S(2)}) copy-start(s32[1,1,1,64,128]{4,3,2,1,0:T(8,128)} %param.17) | copy-start | bytes 98308
  108.9 4.1 copy-start.1
  113.0 1.4 copy-start.2
  122.1 171.6 %reduce-scatter.3.cloned.1.call-start = ((), (), s32[]{:S(2)}) async-start(), calls=%async_computation.6 | async-start | bytes 4718592 | tf_op jit(solution)/shard_map/reduce_scatter | solution.py:90
  132.3 1.0 copy-start.5
  132.3 2.2 copy-start.4
  132.3 3.9 copy-start.13
  132.3 372.9 %all-reduce.19.cloned.1.call-start = ((), (), s32[]{:S(2)}) async-start(), calls=%async_computation.13 | async-start | bytes 262144 | tf_op jit(solution)/shard_map/psum | solution.py:61
  136.1 405.1 %all-reduce.23.cloned.1.call-start = ((), (), s32[]{:S(2)}) async-start(), calls=%async_computation.15 | async-start | bytes 1572864 | tf_op jit(solution)/shard_map/psum | solution.py:92
  295.6 287.3 %all-gather.9.cloned.1.call-start = ((), (), s32[]{:S(2)}) async-start(), calls=%async_computation.7 | async-start | bytes 2359296 | tf_op jit(solution)/shard_map/all_gather | solution.py:80
  541.2 26.7 %copy-start.7 = (f32[128,512]{0,1:T(8,128)S(1)}, f32[128,512]{0,1:T(8,128)}, u32[]{:S(2)}) copy-start(f32[128,512]{0,1:T(8,128)} %get-tuple-element.18) | copy-start | bytes 786436
  544.4 92.8 %all-gather.11.cloned.1.call-start = ((), (), s32[]{:S(2)}) async-start(), calls=%async_computation.8 | async-start | bytes 2228224 | tf_op jit(solution)/shard_map/all_gather | solution.py:81
  569.5 281.0 %all-reduce.17.cloned.1.call-start = ((), (), s32[]{:S(2)}) async-start(), calls=%async_computation.12 | async-start | bytes 262144 | tf_op jit(solution)/shard_map/psum | solution.py:61
  571.8 397.6 %all-reduce.15.cloned.1.call-start = ((), (), s32[]{:S(2)}) async-start(), calls=%async_computation.11 | async-start | bytes 8388608
  639.7 4.1 copy-start
  643.9 1.4 copy-start.3
  652.9 374.5 %reduce-scatter.5.cloned.1.call-start = ((), (), s32[]{:S(2)}) async-start(), calls=%async_computation.9 | async-start | bytes 4718592 | tf_op jit(solution)/shard_map/reduce_scatter | solution.py:90
  663.0 400.3 %all-reduce.21.cloned.1.call-start = ((), (), s32[]{:S(2)}) async-start(), calls=%async_computation.14 | async-start | bytes 1572864 | tf_op jit(solution)/shard_map/psum | solution.py:92
  850.6 189.4 %copy-start.6 = (f32[128,128]{0,1:T(8,128)S(1)}, f32[128,128]{0,1:T(8,128)}, u32[]{:S(2)}) copy-start(f32[128,128]{0,1:T(8,128)} %get-tuple-element.12) | copy-start | bytes 196612
  1063.2 3.3 copy-start.8
Sparse Core Ops, SparseCore 0:
  10.4 41.2 all-gather.4
  54.7 51.5 all-gather.6
  122.2 113.6 all-reduce.12
  238.3 55.3 reduce-scatter.2
  299.1 206.1 all-reduce.18
  508.5 32.6 all-reduce.22
  544.5 38.3 all-gather.8
  585.9 51.1 all-gather.10
  642.7 207.7 all-reduce.16
  854.1 115.2 all-reduce.14
  972.1 55.3 reduce-scatter.4
  1030.7 29.7 all-reduce.20
where the time goes:
time: 1080 us
  waiting for transfers between devices  852 us (79%)
  other arithmetic  99.6 us (9%)
  matrix products  56.4 us (5%)
  local copies, waits for them, and re-layouts  34.4 us (3%)
  starting transfers between devices  17.6 us (2%)
  between operations  15.7 us (1%)
    psum x2, waiting for transfers between devices, on_device(): lax.psum((jnp.dot(users.T, users, precision=lax.Precision.HIGHEST, prefer...  396 us
    unnamed x14, waiting for transfers between devices  203 us
    reduce_scatter x2, waiting for transfers between devices, on_device(): lax.psum_scatter(user_pooled, 'tcol', scatter_dimension=0, tiled=True)  112 us
    all_gather x2, waiting for transfers between devices, on_device(): item_pool = lax.all_gather(item_half, 'trow', axis=0, tiled=True)  101 us
    another operation x12, other arithmetic, precondition(): factor = jnp.linalg.cholesky(gramian)  49.7 us
    another operation x8, other arithmetic, precondition(): return jax.scipy.linalg.cho_solve((factor, True), gradient.T).T  42.1 us
  transfers between devices with their start and end apart: 14, of which 13 were waited for; matrix products, arithmetic and copies ran while one was open for 15% of the time, Pallas kernels for 0%

commit v1 on v0

v1 whole, which is shorter than its diff:
```python
import functools

import jax
import jax.numpy as jnp
from jax import lax
from jax.experimental import pallas as pl
from jax.experimental.pallas import tpu as pltpu
from jax.sharding import PartitionSpec as P

ITERS = 2
TILE = 128
NX = 4
NY = 4
NZ = 8
NXY = NX * NY
LT = 8
RT = 4
NT = 64
CAPL = 4
CAPR = 2
HU = LT // 2
HI = RT // 2
F32 = jnp.float32
BF16 = jnp.bfloat16
HIGHEST = lax.Precision.HIGHEST


def kernel(
    user_coef,
    item_coef,
    tab,
    sends,
    row_mask,
    col_mask,
    users,
    items,
    ratings,
    out_u,
    out_i,
    lists_u,
    lists_i,
    slists_u,
    slists_i,
    x_row,
    y_row,
    x_col,
    tab_u,
    flag_u,
    tab_i,
    flag_i,
    u_cur,
    i_cur,
    rat,
    weights,
    pool_u,
    pool_i,
    errs,
    run_u,
    run_i,
    gmine,
    gsend,
    gsib,
    gz,
    gchunk,
    gxy,
    gsum,
    gfull,
    gother,
    sibs_u,
    sibr_u,
    ring_s,
    ring_r,
    sibs_i,
    sibr_i,
    half_s,
    half_r,
    full_s,
    full_r,
    quarter,
    ah_s,
    ah_r,
    af_s,
    af_r,
    ssem,
    rsem,
    lsem,
):
    trow = lax.axis_index("trow")
    z = lax.axis_index("tcol")
    c = lax.axis_index("rep")
    other = 1 - c
    x = trow // NY
    y = trow % NY
    a = jnp.where(c == 0, x, y)
    b = jnp.where(c == 0, y, x)
    sa = 4 - 3 * c
    sb = 1 + 3 * c

    def cell(oa, ob):
        return ((a + oa) % 4) * sa + ((b + ob) % 4) * sb

    def remote(src, dst, send_sem, recv_sem, where):
        return pltpu.make_async_remote_copy(
            src_ref=src,
            dst_ref=dst,
            send_sem=send_sem,
            recv_sem=recv_sem,
            device_id=where,
            device_id_type=pl.DeviceIdType.MESH,
        )

    def await_bytes(ref, sem):
        pltpu.make_async_copy(ref, ref, sem).wait()

    sibling = {"rep": other}

    load_r = pltpu.make_async_copy(ratings, rat, lsem.at[0])
    load_u = pltpu.make_async_copy(users.at[pl.ds(HU * c, HU)], u_cur, lsem.at[1])
    load_i = pltpu.make_async_copy(items.at[pl.ds(HI * c, HI)], i_cur, lsem.at[2])
    load_u.start()
    load_i.start()
    load_r.start()

    barrier = pltpu.get_barrier_semaphore()
    for d in range(1, NZ):
        pl.semaphore_signal(
            barrier, inc=1, device_id={"tcol": (z + d) % NZ}, device_id_type=pl.DeviceIdType.MESH
        )
    for d in range(1, NXY):
        pl.semaphore_signal(
            barrier,
            inc=1,
            device_id={"trow": (trow + d) % NXY},
            device_id_type=pl.DeviceIdType.MESH,
        )
    pl.semaphore_signal(barrier, inc=1, device_id=sibling, device_id_type=pl.DeviceIdType.MESH)
    pl.semaphore_wait(barrier, NZ - 1 + NXY - 1 + 1)

    for d in range(1, NZ):
        remote(
            sends.at[0], lists_u.at[z], lsem.at[3], lsem.at[4], {"tcol": (z + d) % NZ}
        ).start()
    for d in range(1, NXY):
        remote(
            sends.at[0], lists_i.at[trow], lsem.at[5], lsem.at[6], {"trow": (trow + d) % NXY}
        ).start()
    lists_u[z] = sends[0]
    lists_i[trow] = sends[0]
    load_u.wait()
    load_i.wait()

    lane = lax.broadcasted_iota(jnp.int32, (TILE, TILE), 1)

    def make_weights():
        padded = jnp.concatenate(
            [row_mask[...].astype(F32), jnp.zeros((TILE - NT, TILE), F32)], axis=0
        )
        quarter[0, 0] = padded.T

        def one(t, carry):
            spread = jnp.take_along_axis(
                quarter[0, 0], jnp.full((TILE, TILE), t, jnp.int32), axis=1, mode="promise_in_bounds"
            )
            weights[t] = (spread * col_mask[pl.ds(t, 1), :].astype(F32)).astype(BF16)
            return carry

        lax.fori_loop(0, NT, one, 0)

    def make_tables():
        await_bytes(lists_u.at[pl.ds(0, NZ - 1)], lsem.at[3])
        await_bytes(lists_u.at[pl.ds(0, NZ - 1)], lsem.at[4])
        await_bytes(lists_i.at[pl.ds(0, NXY - 1)], lsem.at[5])
        await_bytes(lists_i.at[pl.ds(0, NXY - 1)], lsem.at[6])
        down_u = pltpu.make_async_copy(lists_u, slists_u, lsem.at[7])
        down_i = pltpu.make_async_copy(lists_i, slists_i, lsem.at[8])
        down_u.start()
        down_i.start()
        down_u.wait()
        down_i.wait()

        def user_tile(slot):
            source = slot // CAPL
            return source * LT + slists_u[source, 0, z * CAPL + slot % CAPL]

        def item_tile(slot):
            source = slot // CAPR
            return source * RT + slists_i[source, 0, NZ * CAPL + trow * CAPR + slot % CAPR]

        def one(k, carry):
            x_row[k] = user_tile(tab[1, k])
            y_row[k] = item_tile(tab[2, k])
            x_col[k] = user_tile(tab[5, k])
            source = k // LT
            found = jnp.int32(-1)
            for s in range(CAPL):
                found = jnp.where(
                    slists_u[source, 0, z * CAPL + s] == k % LT, tab[6, source * CAPL + s], found
                )
            flag_u[k] = jnp.where(found >= 0, 1, 0)
            tab_u[k] = jnp.maximum(found, 0)
            source = k // RT
            found = jnp.int32(-1)
            for s in range(CAPR):
                found = jnp.where(
                    slists_i[source, 0, NZ * CAPL + trow * CAPR + s] == k % RT,
                    tab[7, source * CAPR + s],
                    found,
                )
            flag_i[k] = jnp.where(found >= 0, 1, 0)
            tab_i[k] = jnp.maximum(found, 0)
            return carry

        lax.fori_loop(0, NT, one, 0)

    def iteration(it, carry):
        names = {}
        pending = []

        def number(name):
            names.setdefault(name, len(names))
            return names[name]

        def begin(name, src, dst, where):
            n = number(name)
            copy = remote(src, dst, ssem.at[n], rsem.at[it, n], where)
            copy.start()
            pending.append(copy)

        def arrive(name, ref):
            await_bytes(ref, rsem.at[it, number(name)])

        for l in range(HU):
            pool_u[it, z * LT + HU * c + l] = u_cur[l].astype(BF16)
        for l in range(HI):
            pool_i[it, trow * RT + HI * c + l] = i_cur[l].astype(BF16)

        def pair_u(o, pr):
            return pool_u.at[it, pl.ds(((z + o) % NZ) * LT + HU * c + 2 * pr, 2)]

        def send_u(way, step, pr):
            ref = pair_u(-way * (step - 1) + NZ, pr)
            begin(("u", way, step, pr), ref, ref, {"tcol": (z + way + NZ) % NZ})

        def sib_u(o, pr):
            ref = pair_u(o, pr)
            remote(ref, ref, ssem.at[number("su")], rsem.at[it, number("su")], sibling).start()

        def chunk_i(oa, ob):
            return pool_i.at[it, pl.ds(cell(oa, ob) * RT + HI * c, HI)]

        def tile_i(oa, ob, j):
            return pool_i.at[it, pl.ds(cell(oa, ob) * RT + HI * c + j, 1)]

        def along_a(way):
            return {"trow": cell(way + 4, 0)}

        def along_b(way):
            return {"trow": cell(0, way + 4)}

        def sib_i(oa, ob):
            ref = chunk_i(oa, ob)
            remote(ref, ref, ssem.at[number("si")], rsem.at[it, number("si")], sibling).start()

        def second_i(oa):
            for way in (1, -1):
                begin(("b", way, oa), chunk_i(oa, 0), chunk_i(oa, 0), along_b(way))

        for pr in range(2):
            for way in (1, -1):
                send_u(way, 1, pr)
        for way in (1, -1):
            begin(("a", way), chunk_i(0, 0), chunk_i(0, 0), along_a(way))
        second_i(0)
        for pr in range(2):
            sib_u(0, pr)
        sib_i(0, 0)

        def gram(ref, count):
            flat = ref[...].reshape(count * TILE, TILE)
            return lax.dot_general(
                flat, flat, (((0,), (0,)), ((), ())), precision=HIGHEST, preferred_element_type=F32
            )

        gram_u = gram(u_cur, HU)
        gram_i = gram(i_cur, HI)
        gsend[...] = jnp.where(c == 0, gram_i, gram_u)
        begin("gs", gsend, gsib.at[it], sibling)
        gmine[...] = jnp.where(c == 0, gram_u, gram_i)

        @pl.when(it == 0)
        def _():
            make_weights()

        arrive("gs", gsib.at[it])
        gmine[...] += gsib[it]
        for d in range(1, NZ):
            zz = (z + d) % NZ
            remote(
                gmine.at[pl.ds(16 * zz, 16)],
                gz.at[it, d - 1],
                ssem.at[number("gz")],
                rsem.at[it, number("gz")],
                {"tcol": zz},
            ).start()

        def got_u(way, step, pr):
            arrive(("u", way, step, pr), pair_u(-way * step + NZ, pr))
            if step < 3 or (step == 3 and pr == (0 if way == 1 else 1)):
                send_u(way, step + 1, pr)
            sib_u(-way * step + NZ, pr)

        def first_got(way):
            oa = (4 - way) % 4
            arrive(("a", way), chunk_i(oa, 0))
            j = 0 if way == 1 else 1
            ref = tile_i(oa, 0, j)
            begin(("af", way), ref, ref, along_a(way))
            second_i(oa)
            sib_i(oa, 0)

        def first_far():
            for way, j in ((1, 0), (-1, 1)):
                arrive(("af", way), tile_i(2, 0, j))
            second_i(2)
            sib_i(2, 0)

        def second_got(oa):
            for way, j in ((1, 0), (-1, 1)):
                arrive(("b", way, oa), chunk_i(oa, 4 - way))
                ref = tile_i(oa, 4 - way, j)
                begin(("bf", way, oa), ref, ref, along_b(way))
                sib_i(oa, 4 - way)

        def second_far(oa):
            for way, j in ((1, 0), (-1, 1)):
                arrive(("bf", way, oa), tile_i(oa, 2, j))
            sib_i(oa, 2)

        for pr in range(2):
            for way in (1, -1):
                got_u(way, 1, pr)
        first_got(1)
        first_got(-1)
        second_got(0)
        first_far()
        for pr in range(2):
            for way in (1, -1):
                got_u(way, 2, pr)

        await_bytes(gz.at[it], rsem.at[it, number("gz")])
        total = gmine[pl.ds(16 * z, 16), :]
        for d in range(NZ - 1):
            total = total + gz[it, d]
        gchunk[...] = total
        gxy[it, trow] = total
        for d in range(1, NXY):
            remote(
                gchunk,
                gxy.at[it, trow],
                ssem.at[number("gxy")],
                rsem.at[it, number("gxy")],
                {"trow": (trow + d) % NXY},
            ).start()

        @pl.when(it == 0)
        def _():
            make_tables()

        second_got(3)
        second_got(1)
        for way in (1, -1):
            got_u(way, 3, 0)
        second_far(0)
        for way in (1, -1):
            got_u(way, 3, 1)
        second_got(2)

        await_bytes(gxy.at[it, pl.ds(0, NXY - 1)], rsem.at[it, number("gxy")])
        total = gxy[it, 0]
        for d in range(1, NXY):
            total = total + gxy[it, d]
        gsum[...] = total
        gfull[it, pl.ds(16 * z, 16), :] = total
        for d in range(1, NZ):
            remote(
                gsum,
                gfull.at[it, pl.ds(16 * z, 16)],
                ssem.at[number("gd")],
                rsem.at[it, number("gd")],
                {"tcol": (z + d) % NZ},
            ).start()

        second_far(3)
        second_far(1)
        got_u(1, 4, 0)
        got_u(-1, 4, 1)
        second_far(2)

        @pl.when(it == 0)
        def _():
            load_r.wait()

        await_bytes(pool_u.at[it, pl.ds(0, NT // 2)], rsem.at[it, number("su")])
        await_bytes(pool_i.at[it, pl.ds(0, NT // 2)], rsem.at[it, number("si")])

        def user_pass(k, carry):
            run, before = carry
            t = tab[0, k]
            slot = tab[1, k]
            xt = pool_u[it, x_row[k]]
            yt = pool_i[it, y_row[k]]
            predicted = lax.dot_general(
                xt, yt, (((1,), (1,)), ((), ())), preferred_element_type=F32
            )
            err = ((predicted - rat[t].astype(F32)) * weights[t].astype(F32)).astype(BF16)
            errs[k] = err
            term = jnp.dot(err, yt, preferred_element_type=F32)
            run = jnp.where(slot == before, run, 0.0) + term
            run_u[k] = run
            return run, slot

        zero = jnp.zeros((TILE, TILE), F32)
        lax.fori_loop(0, NT, user_pass, (zero, jnp.int32(-1)), unroll=2)

        def own_u(o, l):
            p = ((z + o) % NZ) * LT + HU * c + l
            return run_u[tab_u[p]] * flag_u[p].astype(F32)

        def share_u(o):
            def one(l, carry):
                p = ((z + o) % NZ) * LT + HU * other + l
                sibs_u[o, l] = (run_u[tab_u[p]] * flag_u[p].astype(F32)).astype(BF16)
                return carry

            lax.fori_loop(0, HU, one, 0)
            begin(("su", o), sibs_u.at[o], sibr_u.at[it, o], sibling)

        for o in (4, 3, 5, 2, 6, 1, 7, 0):
            share_u(o)

        def item_pass(k, carry):
            run, before = carry
            slot = tab[4, k]
            term = lax.dot_general(
                errs[tab[3, k]],
                pool_u[it, x_col[k]],
                (((0,), (0,)), ((), ())),
                preferred_element_type=F32,
            )
            run = jnp.where(slot == before, run, 0.0) + term
            run_i[k] = run
            return run, slot

        def ring_send(w, k, pr):
            ref = ring_s.at[w, k, pl.ds(2 * pr, 2)]
            begin(
                ("r", w, k, pr),
                ref,
                ring_r.at[it, w, k, pl.ds(2 * pr, 2)],
                {"tcol": (z + (1, NZ - 1)[w]) % NZ},
            )

        def ring_first(w):
            for l in (2 * w, 2 * w + 1):
                ring_s[w, 0, l] = (own_u(4, l) + sibr_u[it, 4, l].astype(F32)).astype(BF16)
            ring_send(w, 0, w)

        def ring_step(w, k):
            o = (4 - k) if w == 0 else 4 + k
            arrive(("su", o), sibr_u.at[it, o])
            for pr in (w, 1 - w):
                held = k > 1 or pr == w
                if held:
                    arrive(("r", w, k - 1, pr), ring_r.at[it, w, k - 1, pl.ds(2 * pr, 2)])
                for l in (2 * pr, 2 * pr + 1):
                    value = own_u(o, l) + sibr_u[it, o, l].astype(F32)
                    if held:
                        value = value + ring_r[it, w, k - 1, l].astype(F32)
                    ring_s[w, k, l] = value.astype(BF16)
                ring_send(w, k, pr)

        arrive(("su", 4), sibr_u.at[it, 4])
        ring_first(0)
        ring_first(1)
        lax.fori_loop(0, NT, item_pass, (zero, jnp.int32(-1)), unroll=2)

        def share_i(p, carry):
            q = p * RT + HI * other
            for j in range(HI):
                sibs_i[p, j] = (run_i[tab_i[q + j]] * flag_i[q + j].astype(F32)).astype(BF16)
            return carry

        lax.fori_loop(0, NXY, share_i, 0)
        begin("shi", sibs_i, sibr_i.at[it], sibling)
        ring_step(0, 1)
        ring_step(1, 1)
        arrive("shi", sibr_i.at[it])

        def own_i(oa, ob, j):
            p = cell(oa, ob)
            q = p * RT + HI * c + j
            return run_i[tab_i[q]] * flag_i[q].astype(F32) + sibr_i[it, p, j].astype(F32)

        for w, ob in ((0, 1), (1, 3)):

            def one(o, carry, w=w):
                half_s[w, o] = own_i(o, 2, w).astype(BF16)
                return carry

            lax.fori_loop(0, 4, one, 0)
            begin(("h", w), half_s.at[w], half_r.at[it, w], {"trow": cell(0, ob)})

        await_bytes(gfull.at[it, pl.ds(0, 16 * (NZ - 1))], rsem.at[it, number("gd")])

        def eliminate(k, carry):
            mat = gfull[it]
            row = gfull[it, pl.ds(k, 1), :]
            pick = jnp.full((TILE, TILE), k, jnp.int32)
            column = jnp.take_along_axis(mat, pick, axis=1, mode="promise_in_bounds")
            pivot = gfull[it, pl.ds(k, 1), :]
            pivot = jnp.sum(jnp.where(lane[0:1] == k, pivot, 0.0), axis=1, keepdims=True)
            scaled = jnp.where(lane[0:1] == k, 1.0, row) / pivot
            gfull[it] = jnp.where(lane == k, 0.0, mat) - column * scaled
            gfull[it, pl.ds(k, 1), :] = scaled
            return carry

        def invert(low, high):
            lax.fori_loop(low, high, eliminate, 0)

        invert(0, 32)
        ring_step(0, 2)
        ring_step(1, 2)

        for w, ob in ((0, 1), (1, 3)):
            arrive(("h", w), half_r.at[it, w])

            def one(o, carry, w=w, ob=ob):
                for j in range(HI):
                    value = own_i(o, ob, j)
                    if j == w:
                        value = value + half_r[it, w, o].astype(F32)
                    full_s[w, o, j] = value.astype(BF16)
                return carry

            lax.fori_loop(0, 4, one, 0)
            begin(("f", w), full_s.at[w], full_r.at[it, w], {"trow": cell(0, ob)})

        invert(32, 64)
        ring_step(0, 3)
        ring_step(1, 3)

        for w in range(2):
            arrive(("f", w), full_r.at[it, w])

        def one(o, carry):
            for j in range(HI):
                quarter[o, j] = (
                    own_i(o, 0, j) + full_r[it, 0, o, j].astype(F32) + full_r[it, 1, o, j].astype(F32)
                )
            return carry

        lax.fori_loop(0, 4, one, 0)
        for w, oa in ((0, 1), (1, 3)):
            ah_s[w] = quarter[2, w].astype(BF16)
            begin(("ah", w), ah_s.at[w], ah_r.at[it, w], {"trow": cell(oa, 0)})

        invert(64, 96)

        for w, oa in ((0, 1), (1, 3)):
            arrive(("ah", w), ah_r.at[it, w])
            for j in range(HI):
                value = quarter[oa, j]
                if j == w:
                    value = value + ah_r[it, w].astype(F32)
                af_s[w, j] = value.astype(BF16)
            begin(("af2", w), af_s.at[w], af_r.at[it, w], {"trow": cell(oa, 0)})

        invert(96, TILE)
        begin("inv", gfull.at[it], gother.at[it], sibling)
        arrive(("su", 0), sibr_u.at[it, 0])
        for w in range(2):
            for pr in range(2):
                arrive(("r", w, 3, pr), ring_r.at[it, w, 3, pl.ds(2 * pr, 2)])
        grad_u = jnp.concatenate(
            [
                own_u(0, l)
                + sibr_u[it, 0, l].astype(F32)
                + ring_r[it, 0, 3, l].astype(F32)
                + ring_r[it, 1, 3, l].astype(F32)
                for l in range(HU)
            ],
            axis=0,
        )
        for w in range(2):
            arrive(("af2", w), af_r.at[it, w])
        grad_i = jnp.concatenate(
            [
                quarter[0, j] + af_r[it, 0, j].astype(F32) + af_r[it, 1, j].astype(F32)
                for j in range(HI)
            ],
            axis=0,
        )
        arrive("inv", gother.at[it])
        mine = gfull[it]
        theirs = gother[it]
        inverse_u = jnp.where(c == 0, mine, theirs)
        inverse_i = jnp.where(c == 0, theirs, mine)
        step_u = jnp.dot(grad_u, inverse_i, precision=HIGHEST, preferred_element_type=F32)
        step_i = jnp.dot(grad_i, inverse_u, precision=HIGHEST, preferred_element_type=F32)
        u_cur[...] = u_cur[...] - user_coef * step_u.reshape(HU, TILE, TILE)
        i_cur[...] = i_cur[...] - item_coef * step_i.reshape(HI, TILE, TILE)

        for copy in pending:
            copy.wait_send()
        await_bytes(pool_u.at[it, pl.ds(0, NT // 2)], ssem.at[number("su")])
        await_bytes(pool_i.at[it, pl.ds(0, NT // 2)], ssem.at[number("si")])
        await_bytes(gz.at[it], ssem.at[number("gz")])
        await_bytes(gxy.at[it, pl.ds(0, NXY - 1)], ssem.at[number("gxy")])
        await_bytes(gfull.at[it, pl.ds(0, 16 * (NZ - 1))], ssem.at[number("gd")])
        assert len(names) <= 128, len(names)
        return carry

    lax.fori_loop(0, ITERS, iteration, 0)

    last_u = remote(u_cur, out_u.at[pl.ds(HU * c, HU)], lsem.at[1], lsem.at[7], sibling)
    last_i = remote(i_cur, out_i.at[pl.ds(HI * c, HI)], lsem.at[2], lsem.at[8], sibling)
    last_u.start()
    last_i.start()
    for l in range(HU):
        out_u[HU * c + l] = u_cur[l]
    for l in range(HI):
        out_i[HI * c + l] = i_cur[l]
    last_u.wait()
    last_i.wait()


def slot_order(slots):
    count = slots.shape[0]
    at = lax.broadcasted_iota(jnp.int32, (count, count), 0)
    against = lax.broadcasted_iota(jnp.int32, (count, count), 1)
    mine = slots[:, None]
    theirs = slots[None, :]
    ahead = (theirs < mine) | ((theirs == mine) & (against < at))
    rank = jnp.sum(ahead.astype(jnp.int32), axis=1)
    placed = (rank[:, None] == against).astype(jnp.int32)
    return rank, placed


def on_device(
    users, items, ratings, row_mask, col_mask, row_slots, col_slots, send_users, send_items
):
    own_users = users.shape[0] // TILE
    own_items = items.shape[0] // TILE
    all_users = own_users * TILE * NXY * NZ
    all_items = own_items * TILE * NXY * NZ
    user_coef = 2.0 * all_items * own_users / (TILE * NT * 2)
    item_coef = 2.0 * all_users * own_items / (TILE * NT * 2)
    row_list = row_slots.reshape(-1)
    col_list = col_slots.reshape(-1)
    rank_r, placed_r = slot_order(row_list)
    _, placed_c = slot_order(col_list)
    numbers = jnp.arange(NT, dtype=jnp.int32)
    by_row = jnp.sum(placed_r * numbers[:, None], axis=0)
    rs = jnp.sum(placed_r * row_list[:, None], axis=0)
    rc = jnp.sum(placed_r * col_list[:, None], axis=0)
    epos = jnp.sum(placed_c * rank_r[:, None], axis=0)
    cs = jnp.sum(placed_c * col_list[:, None], axis=0)
    cr = jnp.sum(placed_c * row_list[:, None], axis=0)
    last_r = jnp.sum((row_list[:, None] <= numbers[None, :]).astype(jnp.int32), axis=0) - 1
    last_c = jnp.sum((col_list[:, None] <= numbers[None, :]).astype(jnp.int32), axis=0) - 1
    tab = jnp.stack([by_row, rs, rc, epos, cs, cr, last_r, last_c])
    sends = jnp.concatenate(
        [send_users.reshape(-1), send_items.reshape(-1), jnp.zeros((64,), jnp.int32)]
    ).reshape(1, 1, 128)

    any_spec = pl.BlockSpec(memory_space=pl.ANY)
    vmem_spec = pl.BlockSpec(memory_space=pltpu.VMEM)
    smem_spec = pl.BlockSpec(memory_space=pltpu.SMEM)
    square = (TILE, TILE)
    table = pltpu.SMEM((NT,), jnp.int32)
    out_u, out_i = pl.pallas_call(
        functools.partial(kernel, user_coef, item_coef),
        out_shape=(
            jax.ShapeDtypeStruct((LT,) + square, F32),
            jax.ShapeDtypeStruct((RT,) + square, F32),
        ),
        in_specs=[smem_spec, vmem_spec, vmem_spec, vmem_spec, any_spec, any_spec, any_spec],
        out_specs=(vmem_spec, vmem_spec),
        scratch_shapes=[
            pltpu.VMEM((NZ, 1, 128), jnp.int32),
            pltpu.VMEM((NXY, 1, 128), jnp.int32),
            pltpu.SMEM((NZ, 1, 128), jnp.int32),
            pltpu.SMEM((NXY, 1, 128), jnp.int32),
            table,
            table,
            table,
            table,
            table,
            table,
            table,
            pltpu.VMEM((HU,) + square, F32),
            pltpu.VMEM((HI,) + square, F32),
            pltpu.VMEM((NT,) + square, BF16),
            pltpu.VMEM((NT,) + square, BF16),
            pltpu.VMEM((ITERS, NT) + square, BF16),
            pltpu.VMEM((ITERS, NT) + square, BF16),
            pltpu.VMEM((NT,) + square, BF16),
            pltpu.VMEM((NT,) + square, F32),
            pltpu.VMEM((NT,) + square, F32),
            pltpu.VMEM(square, F32),
            pltpu.VMEM(square, F32),
            pltpu.VMEM((ITERS,) + square, F32),
            pltpu.VMEM((ITERS, NZ - 1, 16, TILE), F32),
            pltpu.VMEM((16, TILE), F32),
            pltpu.VMEM((ITERS, NXY, 16, TILE), F32),
            pltpu.VMEM((16, TILE), F32),
            pltpu.VMEM((ITERS,) + square, F32),
            pltpu.VMEM((ITERS,) + square, F32),
            pltpu.VMEM((NZ, HU) + square, BF16),
            pltpu.VMEM((ITERS, NZ, HU) + square, BF16),
            pltpu.VMEM((2, 4, HU) + square, BF16),
            pltpu.VMEM((ITERS, 2, 4, HU) + square, BF16),
            pltpu.VMEM((NXY, HI) + square, BF16),
            pltpu.VMEM((ITERS, NXY, HI) + square, BF16),
            pltpu.VMEM((2, 4) + square, BF16),
            pltpu.VMEM((ITERS, 2, 4) + square, BF16),
            pltpu.VMEM((2, 4, HI) + square, BF16),
            pltpu.VMEM((ITERS, 2, 4, HI) + square, BF16),
            pltpu.VMEM((4, HI) + square, F32),
            pltpu.VMEM((2,) + square, BF16),
            pltpu.VMEM((ITERS, 2) + square, BF16),
            pltpu.VMEM((2, HI) + square, BF16),
            pltpu.VMEM((ITERS, 2, HI) + square, BF16),
            pltpu.SemaphoreType.DMA((128,)),
            pltpu.SemaphoreType.DMA((ITERS, 128)),
            pltpu.SemaphoreType.DMA((9,)),
        ],
        compiler_params=pltpu.CompilerParams(
            collective_id=0, has_side_effects=True, vmem_limit_bytes=60 * 1024 * 1024
        ),
        name="scaled_gd",
    )(
        tab,
        sends,
        row_mask.reshape(NT, TILE),
        col_mask.reshape(NT, TILE),
        users.reshape((LT,) + square),
        items.reshape((RT,) + square),
        ratings.reshape((NT,) + square),
    )
    return out_u.reshape(users.shape), out_i.reshape(items.shape)


def solution(mesh):
    return jax.shard_map(
        on_device,
        mesh=mesh,
        in_specs=(
            P(("trow", "tcol"), None),
            P(("tcol", "trow"), None),
            P("trow", "tcol", "rep", None, None, None),
            P("trow", "tcol", "rep", None, None),
            P("trow", "tcol", "rep", None, None),
            P("trow", "tcol", "rep", None),
            P("trow", "tcol", "rep", None),
            P("trow", "tcol", "rep", None, None),
            P("trow", "tcol", "rep", None, None),
        ),
        out_specs=(P(("trow", "tcol"), None), P(("tcol", "trow"), None)),
        check_vma=False,
    )
```

time: 1080 us -> 158 us (0.15)
  waiting for transfers between devices: 852 us -> 0 us
  Pallas kernels: 0 us -> 148 us
  other arithmetic: 99.6 us -> 3.21 us
  matrix products: 56.4 us -> 0 us
  local copies, waits for them, and re-layouts: 34.4 us -> 5.83 us
  starting transfers between devices: 17.6 us -> 0 us
  between operations: 15.7 us -> 0.67 us
    psum x4 -> x0, waiting for transfers between devices: 407 us -> none  [the longest x2 396 us: on_device(): lax.psum((jnp.dot(users.T, users, precision=lax.Precision.HIGHEST, prefer...]
    unnamed x14 -> x0, waiting for transfers between devices: 203 us -> none
    pallas_call x0 -> x1, Pallas kernels: none -> 148 us  [on_device(): pl.pallas_call(functools.partial(kernel, user_coef, item_coef), out_shape...]
    all_gather x4 -> x0, waiting for transfers between devices: 122 us -> none  [the longest x2 101 us: on_device(): item_pool = lax.all_gather(item_half, 'trow', axis=0, tiled=True)]
    reduce_scatter x2 -> x0, waiting for transfers between devices: 112 us -> none  [on_device(): lax.psum_scatter(user_pooled, 'tcol', scatter_dimension=0, tiled=True)]
    another operation x20 -> x0, other arithmetic: 91.8 us -> none  [the longest x12 49.7 us: precondition(): factor = jnp.linalg.cholesky(gramian)]
    dot_general x18 -> x0, matrix products: 50.2 us -> none  [the longest x4 19.5 us: pool_sum(): jnp.dot(onehot, lower, preferred_element_type=jnp.float32)]
    all_to_all x2 -> x0, starting transfers between devices: 15.8 us -> none  [the longest x1 8.19 us: on_device(): lax.all_to_all(user_sends, 'tcol', split_axis=0, concat_axis=0, tiled=True)]
  transfers between devices with their start and end apart: 14 -> 0, of which waited for: 13 -> 0; matrix products, arithmetic and copies ran while one was open for 15% -> 0% of each run, Pallas kernels for 0% -> 0%
where the time goes in v1:
time: 158 us
  Pallas kernels  148 us (94%)
  local copies, waits for them, and re-layouts  5.83 us (4%)
  other arithmetic  3.21 us (2%)
    pallas_call x1, Pallas kernels, on_device(): pl.pallas_call(functools.partial(kernel, user_coef, item_coef), out_shape...  148 us
    unnamed x4, local copies, waits for them, and re-layouts  5.05 us

profile of v1, /device:TPU:1, one launch (start us, length us, event | category | flops | bytes accessed | tf_op | source)
XLA Modules:
  0.0 157.8 jit_solution(13315592301116609322)
XLA Ops:
  0.6 0.9 convert_reduce_fusion.3
  1.5 0.9 convert_reduce_fusion.2
  2.5 0.8 convert_reduce_fusion
  3.3 0.6 stack.29.tab
  3.9 0.8 copy.15
  4.6 0.1 reshape.58
  4.7 0.8 copy.16
  5.5 0.1 reshape.59
  5.6 0.6 add_bitcast_fusion.sends
  6.2 148.1 %scaled_gd.1 = (f32[8,128,128]{2,1,0:T(8,128)}, f32[4,128,128]{2,1,0:T(8,128)}) custom-call(s32[8,64]{1,0:T(8,128)} %stack.29.tab, s32[1,1,128]{2,1,0:T(1,128)} %add_bitcast_fusion.sends, s32[64,128]{1,0:T(8,128)} %bitcast.30, s32[64,128]{1,0:T(8,128)} %bitcast.31, f32[8,128,128]{2,1,0:T(8,128)} %bitcast.26, f32[4,128,128]{2,1,0:T(8,128)} %bitcast.28, ...), custom_call_target="tpu_custom_call" | custom-call | tf_op jit(solution)/shard_map/scaled_gd/pallas_call | solution.py:681
  154.3 1.9 %copy.19 = f32[1024,128]{1,0:T(8,128)} copy(f32[1024,128]{1,0:T(8,128)} %bitcast.27) | data formatting | bytes 1048576
  156.1 1.7 %copy.20 = f32[512,128]{1,0:T(8,128)} copy(f32[512,128]{1,0:T(8,128)} %bitcast.29) | data formatting | bytes 524288
  (2 shorter events, 0.0 us)

commit v2 on v1

v2 whole, which is shorter than its diff:
```python
import functools

import jax
import jax.numpy as jnp
from jax import lax
from jax.experimental import pallas as pl
from jax.experimental.pallas import tpu as pltpu
from jax.sharding import PartitionSpec as P

ITERS = 2
TILE = 128
NX = 4
NY = 4
NZ = 8
NXY = NX * NY
LT = 8
RT = 4
NT = 64
CAPL = 4
CAPR = 2
HU = LT // 2
HI = RT // 2
F32 = jnp.float32
BF16 = jnp.bfloat16
HIGHEST = lax.Precision.HIGHEST


def kernel(
    user_coef,
    item_coef,
    row_slots,
    col_slots,
    sends,
    row_mask,
    col_mask,
    users,
    items,
    ratings,
    out_u,
    out_i,
    lists_u,
    lists_i,
    rows_u,
    rows_i,
    slists_u,
    slists_i,
    vtab,
    tab,
    x_row,
    y_row,
    x_col,
    tab_u,
    tab_i,
    u_cur,
    i_cur,
    rat,
    weights,
    pool_u,
    pool_i,
    errs,
    run_u,
    run_i,
    gmine,
    gsend,
    gsib,
    gz,
    gchunk,
    gxy,
    gsum,
    gfull,
    gother,
    sibs_u,
    sibr_u,
    ring_s,
    ring_r,
    sibs_i,
    sibr_i,
    half_s,
    half_r,
    full_s,
    full_r,
    quarter,
    ah_s,
    ah_r,
    af_s,
    af_r,
    ssem,
    rsem,
    lsem,
):
    trow = lax.axis_index("trow")
    z = lax.axis_index("tcol")
    c = lax.axis_index("rep")
    other = 1 - c
    x = trow // NY
    y = trow % NY
    a = jnp.where(c == 0, x, y)
    b = jnp.where(c == 0, y, x)
    sa = 4 - 3 * c
    sb = 1 + 3 * c

    def cell(oa, ob):
        return ((a + oa) % 4) * sa + ((b + ob) % 4) * sb

    def remote(src, dst, send_sem, recv_sem, where):
        return pltpu.make_async_remote_copy(
            src_ref=src,
            dst_ref=dst,
            send_sem=send_sem,
            recv_sem=recv_sem,
            device_id=where,
            device_id_type=pl.DeviceIdType.MESH,
        )

    def await_bytes(ref, sem):
        pltpu.make_async_copy(ref, ref, sem).wait()

    sibling = {"rep": other}

    load_r = pltpu.make_async_copy(ratings, rat, lsem.at[0])
    load_u = pltpu.make_async_copy(users.at[pl.ds(HU * c, HU)], u_cur, lsem.at[1])
    load_i = pltpu.make_async_copy(items.at[pl.ds(HI * c, HI)], i_cur, lsem.at[2])
    load_u.start()
    load_i.start()
    load_r.start()

    barrier = pltpu.get_barrier_semaphore()
    for d in range(1, NZ):
        pl.semaphore_signal(
            barrier, inc=1, device_id={"tcol": (z + d) % NZ}, device_id_type=pl.DeviceIdType.MESH
        )
    for d in range(1, NXY):
        pl.semaphore_signal(
            barrier,
            inc=1,
            device_id={"trow": (trow + d) % NXY},
            device_id_type=pl.DeviceIdType.MESH,
        )
    pl.semaphore_signal(barrier, inc=1, device_id=sibling, device_id_type=pl.DeviceIdType.MESH)
    lane = lax.broadcasted_iota(jnp.int32, (TILE, TILE), 1)

    def mask_columns():
        padded = jnp.concatenate(
            [row_mask[...].astype(F32), jnp.zeros((TILE - NT, TILE), F32)], axis=0
        )
        quarter[0, 0] = padded.T

    def make_weights(low, high):
        def one(t, carry):
            spread = jnp.take_along_axis(
                quarter[0, 0], jnp.full((TILE, TILE), t, jnp.int32), axis=1, mode="promise_in_bounds"
            )
            weights[t] = (spread * col_mask[pl.ds(t, 1), :].astype(F32)).astype(BF16)
            return carry

        lax.fori_loop(low, high, one, 0, unroll=4)

    def order_tiles():
        at = lax.broadcasted_iota(jnp.int32, (NT, NT), 0).astype(F32)
        against = lax.broadcasted_iota(jnp.int32, (NT, NT), 1).astype(F32)

        def upright(row):
            return jnp.sum(jnp.where(at == against, row, 0.0), axis=1, keepdims=True)

        def order(row):
            col = upright(row)
            tied = jnp.where(row == col, jnp.where(against < at, 1.0, 0.0), 0.0)
            rank = jnp.sum(jnp.where(row < col, 1.0, tied), axis=1, keepdims=True)
            return col, rank, jnp.where(rank == against, 1.0, 0.0)

        def nearness(slot):
            o = (lax.shift_right_logical(slot, 2) + NZ - z) & (NZ - 1)
            place = jnp.where(o > 4, 2 * (NZ - o) - 1, 2 * o)
            place = jnp.where(o == 4, 7, place)
            return (CAPL * place + (slot & (CAPL - 1))).astype(F32)

        def along(placed, col):
            return jnp.sum(placed * col, axis=0, keepdims=True)

        lanes = lax.broadcasted_iota(jnp.int32, (1, NT), 1)
        row_key, row_rank, row_placed = order(nearness(row_slots[...]))
        col_col, _, col_placed = order(col_slots[...].astype(F32))
        row_col = upright(row_slots[...].astype(F32))
        row_first = jnp.sum(jnp.where(row_key < nearness(lanes), 1.0, 0.0), axis=0, keepdims=True)
        col_first = jnp.sum(jnp.where(col_col < against, 1.0, 0.0), axis=0, keepdims=True)
        table = jnp.concatenate(
            [
                along(row_placed, at[:, 0:1]),
                along(row_placed, row_col),
                along(row_placed, col_col),
                along(col_placed, row_rank),
                along(col_placed, col_col),
                along(col_placed, row_col),
                row_first,
                col_first,
            ],
            axis=0,
        )
        kind = lax.broadcasted_iota(jnp.int32, (8, TILE), 0)
        largest = jnp.where((kind == 0) | (kind == 3) | (kind > 5), NT - 1, NT // 2 - 1)
        table = jnp.concatenate([table, jnp.zeros((8, TILE - NT), F32)], axis=1)
        vtab[...] = jnp.minimum(jnp.maximum(table.astype(jnp.int32), 0), largest)
        pltpu.make_async_copy(vtab, tab, lsem.at[9]).start()

    def make_tables():
        await_bytes(lists_u.at[pl.ds(0, NZ - 1)], lsem.at[3])
        await_bytes(lists_u.at[pl.ds(0, NZ - 1)], lsem.at[4])
        await_bytes(lists_i.at[pl.ds(0, NXY - 1)], lsem.at[5])
        await_bytes(lists_i.at[pl.ds(0, NXY - 1)], lsem.at[6])
        rows_u[...] = jnp.concatenate(
            [lists_u[s, pl.ds(z, 1), :] for s in range(NZ)], axis=0
        )
        rows_i[...] = jnp.concatenate(
            [lists_i[s, pl.ds(trow, 1), :] for s in range(NXY)], axis=0
        )
        down_u = pltpu.make_async_copy(rows_u, slists_u, lsem.at[7])
        down_i = pltpu.make_async_copy(rows_i, slists_i, lsem.at[8])
        down_u.start()
        down_i.start()

    def finish_tables():
        pltpu.make_async_copy(vtab, tab, lsem.at[9]).wait()
        pltpu.make_async_copy(rows_u, slists_u, lsem.at[7]).wait()
        pltpu.make_async_copy(rows_i, slists_i, lsem.at[8]).wait()

        def user_tile(slot):
            source = slot // CAPL
            return source * LT + slists_u[source, slot % CAPL]

        def item_tile(slot):
            source = slot // CAPR
            return source * RT + slists_i[source, slot % CAPR]

        def one(k, carry):
            x_row[k] = user_tile(tab[1, k])
            y_row[k] = item_tile(tab[2, k])
            x_col[k] = user_tile(tab[5, k])
            source = k // LT
            found = jnp.int32(NT)
            for s in range(CAPL):
                found = jnp.where(
                    slists_u[source, s] == k % LT, tab[6, source * CAPL + s], found
                )
            tab_u[k] = found
            source = k // RT
            found = jnp.int32(NT)
            for s in range(CAPR):
                found = jnp.where(
                    slists_i[source, s] == k % RT,
                    tab[7, source * CAPR + s],
                    found,
                )
            tab_i[k] = found
            return carry

        lax.fori_loop(0, NT, one, 0, unroll=2)
        run_u[NT] = jnp.zeros((TILE, TILE), F32)
        run_i[NT] = jnp.zeros((TILE, TILE), F32)

    order_tiles()
    mask_columns()
    make_weights(0, NT)
    load_u.wait()
    load_i.wait()
    pl.semaphore_wait(barrier, NZ - 1 + NXY - 1 + 1)

    names = {}

    def build(it):
        pending = []

        def number(name):
            names.setdefault(name, len(names))
            return names[name]

        def begin(name, src, dst, where):
            n = number(name)
            copy = remote(src, dst, ssem.at[it, n], rsem.at[it, n], where)
            copy.start()
            pending.append(copy)

        def arrive(name, ref):
            await_bytes(ref, rsem.at[it, number(name)])

        def pair_u(o, pr):
            return pool_u.at[it, pl.ds(((z + o) % NZ) * LT + HU * c + 2 * pr, 2)]

        def send_u(way, step, pr):
            ref = pair_u(-way * (step - 1) + NZ, pr)
            begin(("u", way, step, pr), ref, ref, {"tcol": (z + way + NZ) % NZ})

        def sib_u(o, pr):
            ref = pair_u(o, pr)
            n = number(("sg", o % NZ))
            remote(ref, ref, ssem.at[it, n], rsem.at[it, n], sibling).start()

        def other_u(o):
            return pool_u.at[it, pl.ds(((z + o) % NZ) * LT + HU * other, HU)]

        def chunk_i(oa, ob):
            return pool_i.at[it, pl.ds(cell(oa, ob) * RT + HI * c, HI)]

        def tile_i(oa, ob, j):
            return pool_i.at[it, pl.ds(cell(oa, ob) * RT + HI * c + j, 1)]

        def along_a(way):
            return {"trow": cell(way + 4, 0)}

        def along_b(way):
            return {"trow": cell(0, way + 4)}

        def sib_i(oa, ob):
            ref = chunk_i(oa, ob)
            n = number("si")
            remote(ref, ref, ssem.at[it, n], rsem.at[it, n], sibling).start()

        def second_i(oa):
            for way in (1, -1):
                begin(("b", way, oa), chunk_i(oa, 0), chunk_i(oa, 0), along_b(way))

        def start_users():
            for l in range(HU):
                pool_u[it, z * LT + HU * c + l] = u_cur[l].astype(BF16)
            for pr in range(2):
                for way in (1, -1):
                    send_u(way, 1, pr)
            for pr in range(2):
                sib_u(0, pr)

        def start_items():
            for l in range(HI):
                pool_i[it, trow * RT + HI * c + l] = i_cur[l].astype(BF16)
            for way in (1, -1):
                begin(("a", way), chunk_i(0, 0), chunk_i(0, 0), along_a(way))
            second_i(0)
            sib_i(0, 0)

        def gram(ref, count):
            flat = ref[...].reshape(count * TILE, TILE)
            return lax.dot_general(
                flat, flat, (((0,), (0,)), ((), ())), precision=HIGHEST, preferred_element_type=F32
            )

        def start_gram():
            gram_u = gram(u_cur, HU)
            gram_i = gram(i_cur, HI)
            gsend[...] = jnp.where(c == 0, gram_i, gram_u)
            begin("gs", gsend, gsib.at[it], sibling)
            gmine[...] = jnp.where(c == 0, gram_u, gram_i)

        def gram_along_z():
            arrive("gs", gsib.at[it])
            gmine[...] += gsib[it]
            for d in range(1, NZ):
                zz = (z + d) % NZ
                remote(
                    gmine.at[pl.ds(16 * zz, 16)],
                    gz.at[it, d - 1],
                    ssem.at[it, number("gz")],
                    rsem.at[it, number("gz")],
                    {"tcol": zz},
                ).start()

        def gram_across():
            await_bytes(gz.at[it], rsem.at[it, number("gz")])
            total = gmine[pl.ds(16 * z, 16), :]
            for d in range(NZ - 1):
                total = total + gz[it, d]
            gchunk[...] = total
            gxy[it, trow] = total
            for d in range(1, NXY):
                remote(
                    gchunk,
                    gxy.at[it, trow],
                    ssem.at[it, number("gxy")],
                    rsem.at[it, number("gxy")],
                    {"trow": (trow + d) % NXY},
                ).start()

        def gram_whole():
            await_bytes(gxy.at[it, pl.ds(0, NXY - 1)], rsem.at[it, number("gxy")])
            total = gxy[it, 0]
            for d in range(1, NXY):
                total = total + gxy[it, d]
            gsum[...] = total
            gfull[it, pl.ds(16 * z, 16), :] = total
            for d in range(1, NZ):
                remote(
                    gsum,
                    gfull.at[it, pl.ds(16 * z, 16)],
                    ssem.at[it, number("gd")],
                    rsem.at[it, number("gd")],
                    {"tcol": (z + d) % NZ},
                ).start()

        def got_u(way, step, pr):
            arrive(("u", way, step, pr), pair_u(-way * step + NZ, pr))
            if step < 3 or (step == 3 and pr == (0 if way == 1 else 1)):
                send_u(way, step + 1, pr)
            sib_u(-way * step + NZ, pr)

        def first_got(way):
            oa = (4 - way) % 4
            arrive(("a", way), chunk_i(oa, 0))
            j = 0 if way == 1 else 1
            ref = tile_i(oa, 0, j)
            begin(("af", way), ref, ref, along_a(way))
            second_i(oa)
            sib_i(oa, 0)

        def first_far():
            for way, j in ((1, 0), (-1, 1)):
                arrive(("af", way), tile_i(2, 0, j))
            second_i(2)
            sib_i(2, 0)

        def second_got(oa):
            for way, j in ((1, 0), (-1, 1)):
                arrive(("b", way, oa), chunk_i(oa, 4 - way))
                ref = tile_i(oa, 4 - way, j)
                begin(("bf", way, oa), ref, ref, along_b(way))
                sib_i(oa, 4 - way)

        def second_far(oa):
            for way, j in ((1, 0), (-1, 1)):
                arrive(("bf", way, oa), tile_i(oa, 2, j))
            sib_i(oa, 2)

        def at_first(job):
            if it == 0:
                job()

        def error_pass(k, carry):
            t = tab[0, k]
            predicted = lax.dot_general(
                pool_u[it, x_row[k]],
                pool_i[it, y_row[k]],
                (((1,), (1,)), ((), ())),
                preferred_element_type=F32,
            )
            errs[k] = ((predicted - rat[t].astype(F32)) * weights[t].astype(F32)).astype(BF16)
            return carry

        def gather():
            start_gram()
            gram_along_z()
            for pr in range(2):
                for way in (1, -1):
                    got_u(way, 1, pr)
            first_got(1)
            first_got(-1)
            second_got(0)
            at_first(make_tables)
            first_far()
            for pr in range(2):
                for way in (1, -1):
                    got_u(way, 2, pr)
            second_got(3)
            second_got(1)
            second_far(0)
            for way in (1, -1):
                got_u(way, 3, 0)
            gram_across()
            second_got(2)
            for way in (1, -1):
                got_u(way, 3, 1)
            second_far(3)
            second_far(1)
            second_far(2)
            at_first(finish_tables)
            at_first(load_r.wait)
            arrive("si", pool_i.at[it, pl.ds(0, NT // 2)])
            got_u(1, 4, 0)
            got_u(-1, 4, 1)
            for o in range(NZ):
                arrive(("sg", o), other_u(o))
            lax.fori_loop(0, NT, error_pass, 0, unroll=8)

        zero = jnp.zeros((TILE, TILE), F32)

        def item_pass(n, carry):
            k = NT - 1 - n
            run, before = carry
            slot = tab[4, k]
            term = lax.dot_general(
                errs[tab[3, k]],
                pool_u[it, x_col[k]],
                (((0,), (0,)), ((), ())),
                preferred_element_type=F32,
            )
            run = jnp.where(slot == before, run, 0.0) + term
            run_i[k] = run
            return run, slot

        def share_i(ob):
            def one(oa, carry, ob=ob):
                p = ((b + oa) % 4) * sb + ((a + ob) % 4) * sa
                q = p * RT + HI * other
                for j in range(HI):
                    sibs_i[ob, oa, j] = run_i[tab_i[q + j]].astype(BF16)
                return carry

            lax.fori_loop(0, 4, one, 0)
            begin(("shi", ob), sibs_i.at[ob], sibr_i.at[it, ob], sibling)

        def user_pass(n, carry):
            k = NT - 1 - n
            run, before = carry
            slot = tab[1, k]
            term = jnp.dot(errs[k], pool_i[it, y_row[k]], preferred_element_type=F32)
            run = jnp.where(slot == before, run, 0.0) + term
            run_u[k] = run
            return run, slot

        def terms():
            lax.fori_loop(0, NT, item_pass, (zero, jnp.int32(-1)), unroll=8)
            for ob in (2, 1, 3, 0):
                share_i(ob)
            carry = lax.fori_loop(0, 36, user_pass, (zero, jnp.int32(-1)), unroll=6)
            share_u(4)
            for n, o in enumerate((3, 5, 2, 6, 1, 7, 0)):
                carry = lax.fori_loop(36 + 4 * n, 40 + 4 * n, user_pass, carry, unroll=4)
                share_u(o)

        def own_u(o, l):
            p = ((z + o) % NZ) * LT + HU * c + l
            return run_u[tab_u[p]]

        def share_u(o):
            def one(l, carry):
                p = ((z + o) % NZ) * LT + HU * other + l
                sibs_u[o, l] = run_u[tab_u[p]].astype(BF16)
                return carry

            lax.fori_loop(0, HU, one, 0)
            begin(("su", o), sibs_u.at[o], sibr_u.at[it, o], sibling)

        def ring_send(w, k, pr):
            ref = ring_s.at[w, k, pl.ds(2 * pr, 2)]
            begin(
                ("r", w, k, pr),
                ref,
                ring_r.at[it, w, k, pl.ds(2 * pr, 2)],
                {"tcol": (z + (1, NZ - 1)[w]) % NZ},
            )

        def ring_first(w):
            for l in (2 * w, 2 * w + 1):
                ring_s[w, 0, l] = (own_u(4, l) + sibr_u[it, 4, l].astype(F32)).astype(BF16)
            ring_send(w, 0, w)

        def ring_pair(w, k, pr, held):
            o = (4 - k) if w == 0 else 4 + k
            if held:
                arrive(("r", w, k - 1, pr), ring_r.at[it, w, k - 1, pl.ds(2 * pr, 2)])
            for l in (2 * pr, 2 * pr + 1):
                value = own_u(o, l) + sibr_u[it, o, l].astype(F32)
                if held:
                    value = value + ring_r[it, w, k - 1, l].astype(F32)
                ring_s[w, k, l] = value.astype(BF16)
            ring_send(w, k, pr)

        def ring_second(w):
            o = (3, 5)[w]
            arrive(("su", o), sibr_u.at[it, o])
            ring_pair(w, 1, 1 - w, False)

        def ring_step(w, k):
            o = (4 - k) if w == 0 else 4 + k
            if k > 1:
                arrive(("su", o), sibr_u.at[it, o])
                ring_pair(w, k, 1 - w, True)
            ring_pair(w, k, w, True)

        def own_i(oa, ob, j):
            p = cell(oa, ob)
            q = p * RT + HI * c + j
            return run_i[tab_i[q]] + sibr_i[it, ob, oa, j].astype(F32)

        def half_b():
            arrive(("shi", 2), sibr_i.at[it, 2])
            for w, ob in ((0, 1), (1, 3)):

                def one(o, carry, w=w):
                    half_s[w, o] = own_i(o, 2, w).astype(BF16)
                    return carry

                lax.fori_loop(0, 4, one, 0)
                begin(("h", w), half_s.at[w], half_r.at[it, w], {"trow": cell(0, ob)})

        def eliminate(k, carry):
            mat = gfull[it]
            row = gfull[it, pl.ds(k, 1), :]
            pick = jnp.full((TILE, TILE), k, jnp.int32)
            column = jnp.take_along_axis(mat, pick, axis=1, mode="promise_in_bounds")
            pivot = jnp.sum(jnp.where(lane[0:1] == k, row, 0.0), axis=1, keepdims=True)
            scaled = jnp.where(lane[0:1] == k, 1.0, row) / pivot
            gfull[it] = jnp.where(lane == k, 0.0, mat) - column * scaled
            gfull[it, pl.ds(k, 1), :] = scaled
            return carry

        def invert(low, high):
            lax.fori_loop(low, high, eliminate, 0)

        def fold_b(w, ob):
            arrive(("h", w), half_r.at[it, w])
            arrive(("shi", ob), sibr_i.at[it, ob])

            def one(o, carry):
                for j in range(HI):
                    value = own_i(o, ob, j)
                    if j == w:
                        value = value + half_r[it, w, o].astype(F32)
                    full_s[w, o, j] = value.astype(BF16)
                return carry

            lax.fori_loop(0, 4, one, 0)
            for o in (2, 1, 3, 0):
                begin(
                    ("f", w, o), full_s.at[w, o], full_r.at[it, w, o], {"trow": cell(0, ob)}
                )

        def take_b(o):
            for w in range(2):
                arrive(("f", w, o), full_r.at[it, w, o])
            for j in range(HI):
                quarter[o, j] = (
                    own_i(o, 0, j) + full_r[it, 0, o, j].astype(F32) + full_r[it, 1, o, j].astype(F32)
                )

        def half_a():
            for w, oa in ((0, 1), (1, 3)):
                ah_s[w] = quarter[2, w].astype(BF16)
                begin(("ah", w), ah_s.at[w], ah_r.at[it, w], {"trow": cell(oa, 0)})

        def fold_a():
            for w, oa in ((0, 1), (1, 3)):
                arrive(("ah", w), ah_r.at[it, w])
                for j in range(HI):
                    value = quarter[oa, j]
                    if j == w:
                        value = value + ah_r[it, w].astype(F32)
                    af_s[w, j] = value.astype(BF16)
                begin(("af2", w), af_s.at[w], af_r.at[it, w], {"trow": cell(oa, 0)})

        def reduce(after_users, after_items):
            half_b()
            arrive(("su", 4), sibr_u.at[it, 4])
            ring_first(0)
            ring_first(1)
            ring_second(0)
            ring_second(1)
            await_bytes(gfull.at[it, pl.ds(0, 16 * (NZ - 1))], rsem.at[it, number("gd")])
            invert(0, 8)
            ring_step(0, 1)
            ring_step(1, 1)
            fold_b(0, 1)
            fold_b(1, 3)
            invert(8, 24)
            ring_step(0, 2)
            ring_step(1, 2)
            arrive(("shi", 0), sibr_i.at[it, 0])
            take_b(2)
            half_a()
            take_b(1)
            take_b(3)
            invert(24, 40)
            ring_step(0, 3)
            ring_step(1, 3)
            fold_a()
            take_b(0)
            invert(40, TILE)
            finish(after_users, after_items)

        def finish(after_users, after_items):
            begin("inv", gfull.at[it], gother.at[it], sibling)
            arrive(("su", 0), sibr_u.at[it, 0])
            for w in range(2):
                for pr in range(2):
                    arrive(("r", w, 3, pr), ring_r.at[it, w, 3, pl.ds(2 * pr, 2)])
            grad_u = jnp.concatenate(
                [
                    own_u(0, l)
                    + sibr_u[it, 0, l].astype(F32)
                    + ring_r[it, 0, 3, l].astype(F32)
                    + ring_r[it, 1, 3, l].astype(F32)
                    for l in range(HU)
                ],
                axis=0,
            )
            arrive("inv", gother.at[it])
            inverse_i = jnp.where(c == 0, gother[it], gfull[it])
            step_u = jnp.dot(grad_u, inverse_i, precision=HIGHEST, preferred_element_type=F32)
            u_cur[...] = u_cur[...] - user_coef * step_u.reshape(HU, TILE, TILE)
            after_users()
            for w in range(2):
                arrive(("af2", w), af_r.at[it, w])
            grad_i = jnp.concatenate(
                [
                    quarter[0, j] + af_r[it, 0, j].astype(F32) + af_r[it, 1, j].astype(F32)
                    for j in range(HI)
                ],
                axis=0,
            )
            inverse_u = jnp.where(c == 0, gfull[it], gother[it])
            step_i = jnp.dot(grad_i, inverse_u, precision=HIGHEST, preferred_element_type=F32)
            i_cur[...] = i_cur[...] - item_coef * step_i.reshape(HI, TILE, TILE)
            after_items()

        def drain():
            for copy in pending:
                copy.wait_send()
            for o in range(NZ):
                await_bytes(other_u(o), ssem.at[it, number(("sg", o))])
            await_bytes(pool_i.at[it, pl.ds(0, NT // 2)], ssem.at[it, number("si")])
            await_bytes(gz.at[it], ssem.at[it, number("gz")])
            await_bytes(gxy.at[it, pl.ds(0, NXY - 1)], ssem.at[it, number("gxy")])
            await_bytes(gfull.at[it, pl.ds(0, 16 * (NZ - 1))], ssem.at[it, number("gd")])
            assert len(names) <= 128, len(names)

        return start_users, start_items, gather, gram_whole, terms, reduce, drain

    def send_lists():
        for d in range(1, NZ):
            remote(
                sends.at[pl.ds(0, NZ)], lists_u.at[z], lsem.at[3], lsem.at[4], {"tcol": (z + d) % NZ}
            ).start()
        for d in range(1, NXY):
            remote(
                sends.at[pl.ds(NZ, NXY)],
                lists_i.at[trow],
                lsem.at[5],
                lsem.at[6],
                {"trow": (trow + d) % NXY},
            ).start()
        lists_u[z] = sends[0:NZ, :]
        lists_i[trow] = sends[NZ : NZ + NXY, :]

    last_u = remote(u_cur, out_u.at[pl.ds(HU * c, HU)], lsem.at[1], lsem.at[7], sibling)
    last_i = remote(i_cur, out_i.at[pl.ds(HI * c, HI)], lsem.at[2], lsem.at[8], sibling)
    phases = [build(it) for it in range(ITERS)]
    phases[0][0]()
    phases[0][1]()
    send_lists()
    for it in range(ITERS):
        _, _, gather, gram_whole, terms, reduce, drain = phases[it]
        gather()
        gram_whole()
        terms()
        if it + 1 < ITERS:
            reduce(phases[it + 1][0], phases[it + 1][1])
        else:
            reduce(last_u.start, last_i.start)
        drain()

    for l in range(HU):
        out_u[HU * c + l] = u_cur[l]
    for l in range(HI):
        out_i[HI * c + l] = i_cur[l]
    last_u.wait()
    last_i.wait()


def write_out(new_u, new_i, out_u, out_i, sems):
    put_u = pltpu.make_async_copy(new_u, out_u, sems.at[0])
    put_i = pltpu.make_async_copy(new_i, out_i, sems.at[1])
    put_u.start()
    put_i.start()
    put_u.wait()
    put_i.wait()


def on_device(
    users, items, ratings, row_mask, col_mask, row_slots, col_slots, send_users, send_items
):
    own_users = users.shape[0] // TILE
    own_items = items.shape[0] // TILE
    all_users = own_users * TILE * NXY * NZ
    all_items = own_items * TILE * NXY * NZ
    user_coef = 2.0 * all_items * own_users / (TILE * NT * 2)
    item_coef = 2.0 * all_users * own_items / (TILE * NT * 2)
    sends = jnp.concatenate(
        [
            jnp.pad(send_users.reshape(NZ, CAPL), ((0, 0), (0, TILE - CAPL))),
            jnp.pad(send_items.reshape(NXY, CAPR), ((0, 0), (0, TILE - CAPR))),
        ],
        axis=0,
    )

    any_spec = pl.BlockSpec(memory_space=pl.ANY)
    vmem_spec = pl.BlockSpec(memory_space=pltpu.VMEM)
    square = (TILE, TILE)
    table = pltpu.SMEM((NT,), jnp.int32)
    out_u, out_i = pl.pallas_call(
        functools.partial(kernel, user_coef, item_coef),
        out_shape=(
            jax.ShapeDtypeStruct((LT,) + square, F32),
            jax.ShapeDtypeStruct((RT,) + square, F32),
        ),
        in_specs=[vmem_spec] * 5 + [any_spec] * 3,
        out_specs=(vmem_spec, vmem_spec),
        scratch_shapes=[
            pltpu.VMEM((NZ, NZ, TILE), jnp.int32),
            pltpu.VMEM((NXY, NXY, TILE), jnp.int32),
            pltpu.VMEM((NZ, TILE), jnp.int32),
            pltpu.VMEM((NXY, TILE), jnp.int32),
            pltpu.SMEM((NZ, TILE), jnp.int32),
            pltpu.SMEM((NXY, TILE), jnp.int32),
            pltpu.VMEM((8, TILE), jnp.int32),
            pltpu.SMEM((8, TILE), jnp.int32),
            table,
            table,
            table,
            table,
            table,
            pltpu.VMEM((HU,) + square, F32),
            pltpu.VMEM((HI,) + square, F32),
            pltpu.VMEM((NT,) + square, BF16),
            pltpu.VMEM((NT,) + square, BF16),
            pltpu.VMEM((ITERS, NT) + square, BF16),
            pltpu.VMEM((ITERS, NT) + square, BF16),
            pltpu.VMEM((NT,) + square, BF16),
            pltpu.VMEM((NT + 1,) + square, F32),
            pltpu.VMEM((NT + 1,) + square, F32),
            pltpu.VMEM(square, F32),
            pltpu.VMEM(square, F32),
            pltpu.VMEM((ITERS,) + square, F32),
            pltpu.VMEM((ITERS, NZ - 1, 16, TILE), F32),
            pltpu.VMEM((16, TILE), F32),
            pltpu.VMEM((ITERS, NXY, 16, TILE), F32),
            pltpu.VMEM((16, TILE), F32),
            pltpu.VMEM((ITERS,) + square, F32),
            pltpu.VMEM((ITERS,) + square, F32),
            pltpu.VMEM((NZ, HU) + square, BF16),
            pltpu.VMEM((ITERS, NZ, HU) + square, BF16),
            pltpu.VMEM((2, 4, HU) + square, BF16),
            pltpu.VMEM((ITERS, 2, 4, HU) + square, BF16),
            pltpu.VMEM((4, 4, HI) + square, BF16),
            pltpu.VMEM((ITERS, 4, 4, HI) + square, BF16),
            pltpu.VMEM((2, 4) + square, BF16),
            pltpu.VMEM((ITERS, 2, 4) + square, BF16),
            pltpu.VMEM((2, 4, HI) + square, BF16),
            pltpu.VMEM((ITERS, 2, 4, HI) + square, BF16),
            pltpu.VMEM((4, HI) + square, F32),
            pltpu.VMEM((2,) + square, BF16),
            pltpu.VMEM((ITERS, 2) + square, BF16),
            pltpu.VMEM((2, HI) + square, BF16),
            pltpu.VMEM((ITERS, 2, HI) + square, BF16),
            pltpu.SemaphoreType.DMA((ITERS, 128)),
            pltpu.SemaphoreType.DMA((ITERS, 128)),
            pltpu.SemaphoreType.DMA((10,)),
        ],
        compiler_params=pltpu.CompilerParams(
            collective_id=0, has_side_effects=True, vmem_limit_bytes=60 * 1024 * 1024
        ),
        name="scaled_gd",
    )(
        row_slots.reshape(1, NT),
        col_slots.reshape(1, NT),
        sends,
        row_mask.reshape(NT, TILE),
        col_mask.reshape(NT, TILE),
        users.reshape((LT,) + square),
        items.reshape((RT,) + square),
        ratings.reshape((NT,) + square),
    )
    out_u, out_i = pl.pallas_call(
        write_out,
        out_shape=(
            jax.ShapeDtypeStruct((LT,) + square, F32),
            jax.ShapeDtypeStruct((RT,) + square, F32),
        ),
        in_specs=[vmem_spec, vmem_spec],
        out_specs=(any_spec, any_spec),
        scratch_shapes=[pltpu.SemaphoreType.DMA((2,))],
        name="write_out",
    )(out_u, out_i)
    return out_u.reshape(users.shape), out_i.reshape(items.shape)


def solution(mesh):
    return jax.shard_map(
        on_device,
        mesh=mesh,
        in_specs=(
            P(("trow", "tcol"), None),
            P(("tcol", "trow"), None),
            P("trow", "tcol", "rep", None, None, None),
            P("trow", "tcol", "rep", None, None),
            P("trow", "tcol", "rep", None, None),
            P("trow", "tcol", "rep", None),
            P("trow", "tcol", "rep", None),
            P("trow", "tcol", "rep", None, None),
            P("trow", "tcol", "rep", None, None),
        ),
        out_specs=(P(("trow", "tcol"), None), P(("tcol", "trow"), None)),
        check_vma=False,
    )
```

time: 158 us -> 129 us (0.82)
  Pallas kernels: 148 us -> 126 us
  local copies, waits for them, and re-layouts: 5.83 us -> 1.51 us
  other arithmetic: 3.21 us -> 0.61 us
    pallas_call x1, Pallas kernels: 148 us -> 124 us  [on_device(): pl.pallas_call(functools.partial(kernel, user_coef, item_coef), out_shape...]
    unnamed x4 -> x0, local copies, waits for them, and re-layouts: 5.05 us -> none
    reduce_sum x3 -> x0, other arithmetic: 2.62 us -> none  [the longest x2 1.83 us: slot_order(): rank = jnp.sum(ahead.astype(jnp.int32), axis=1)]
    pallas_call x0 -> x1, Pallas kernels: none -> 2 us  [on_device(): pl.pallas_call(write_out, out_shape=(jax.ShapeDtypeStruct((LT,) + square,...]
where the time goes in v2:
time: 129 us
  Pallas kernels  126 us (98%)
  local copies, waits for them, and re-layouts  1.51 us (1%)
    pallas_call x1, Pallas kernels, on_device(): pl.pallas_call(functools.partial(kernel, user_coef, item_coef), out_shape...  124 us

profile of v2, /device:TPU:1, one launch (start us, length us, event | category | flops | bytes accessed | tf_op | source)
XLA Modules:
  0.0 129.0 jit_solution(11002841213681058916)
XLA Ops:
  0.6 0.8 copy.11
  1.4 0.8 copy.12
  2.1 0.6 pad_add_fusion.sends
  2.7 124.3 %scaled_gd.1 = (f32[8,128,128]{2,1,0:T(8,128)}, f32[4,128,128]{2,1,0:T(8,128)}) custom-call(s32[1,64]{1,0:T(1,128)} %bitcast.18, s32[1,64]{1,0:T(1,128)} %bitcast.19, s32[24,128]{1,0:T(8,128)} %pad_add_fusion.sends, s32[64,128]{1,0:T(8,128)} %bitcast.14, s32[64,128]{1,0:T(8,128)} %bitcast.15, f32[8,128,128]{2,1,0:T(8,128)} %bitcast.12, ...), custom_call_target="tpu_custom_call" | custom-call | tf_op jit(solution)/shard_map/scaled_gd/pallas_call | solution.py:794
  127.0 2.0 %write_out.1 = (f32[8,128,128]{2,1,0:T(8,128)}, f32[4,128,128]{2,1,0:T(8,128)}) custom-call(f32[8,128,128]{2,1,0:T(8,128)} %get-tuple-element.6.new_u, f32[4,128,128]{2,1,0:T(8,128)} %get-tuple-element.7.new_i), custom_call_target="tpu_custom_call" | custom-call | tf_op jit(solution)/shard_map/write_out/pallas_call | solution.py:867

commit v3 on v2

--- a/solution.py
+++ b/solution.py
@@ -137,7 +137,7 @@
             device_id_type=pl.DeviceIdType.MESH,
         )
     pl.semaphore_signal(barrier, inc=1, device_id=sibling, device_id_type=pl.DeviceIdType.MESH)
-    lane = lax.broadcasted_iota(jnp.int32, (TILE, TILE), 1)
+    lane8 = lax.broadcasted_iota(jnp.int32, (8, TILE), 1)
 
     def mask_columns():
         padded = jnp.concatenate(
@@ -474,7 +474,9 @@
             got_u(-1, 4, 1)
             for o in range(NZ):
                 arrive(("sg", o), other_u(o))
-            lax.fori_loop(0, NT, error_pass, 0, unroll=8)
+            lax.fori_loop(0, 16, error_pass, 0, unroll=8)
+            gram_whole()
+            lax.fori_loop(16, NT, error_pass, 0, unroll=8)
 
         zero = jnp.zeros((TILE, TILE), F32)
 
@@ -516,7 +518,7 @@
             lax.fori_loop(0, NT, item_pass, (zero, jnp.int32(-1)), unroll=8)
             for ob in (2, 1, 3, 0):
                 share_i(ob)
-            carry = lax.fori_loop(0, 36, user_pass, (zero, jnp.int32(-1)), unroll=6)
+            carry = lax.fori_loop(0, 36, user_pass, (zero, jnp.int32(-1)), unroll=9)
             share_u(4)
             for n, o in enumerate((3, 5, 2, 6, 1, 7, 0)):
                 carry = lax.fori_loop(36 + 4 * n, 40 + 4 * n, user_pass, carry, unroll=4)
@@ -588,15 +590,38 @@
                 lax.fori_loop(0, 4, one, 0)
                 begin(("h", w), half_s.at[w], half_r.at[it, w], {"trow": cell(0, ob)})
 
-        def eliminate(k, carry):
-            mat = gfull[it]
-            row = gfull[it, pl.ds(k, 1), :]
-            pick = jnp.full((TILE, TILE), k, jnp.int32)
-            column = jnp.take_along_axis(mat, pick, axis=1, mode="promise_in_bounds")
-            pivot = jnp.sum(jnp.where(lane[0:1] == k, row, 0.0), axis=1, keepdims=True)
-            scaled = jnp.where(lane[0:1] == k, 1.0, row) / pivot
-            gfull[it] = jnp.where(lane == k, 0.0, mat) - column * scaled
-            gfull[it, pl.ds(k, 1), :] = scaled
+        def eliminate(n, carry):
+            k = 2 * n
+            mat = gfull[it].reshape(16, 8, TILE)
+            row0 = jnp.broadcast_to(gfull[it, pl.ds(k, 1), :], (8, TILE))
+            row1 = jnp.broadcast_to(gfull[it, pl.ds(k + 1, 1), :], (8, TILE))
+            at0 = jnp.full((8, TILE), k, jnp.int32)
+
+            def spread(value, at):
+                return jnp.take_along_axis(value, at, axis=1, mode="promise_in_bounds")
+
+            p = spread(row0, at0)
+            q = spread(row0, at0 + 1)
+            r = spread(row1, at0 + 1)
+            inv_p = 1.0 / p
+            t = q * inv_p
+            inv_s = 1.0 / (r - q * t)
+            here0 = lane8 == k
+            here1 = lane8 == k + 1
+            row0 = jnp.where(here0, 1.0, jnp.where(here1, 0.0, row0))
+            row1 = jnp.where(here1, 1.0, jnp.where(here0, 0.0, row1))
+            new1 = (row1 - t * row0) * inv_s
+            new0 = row0 * inv_p - t * new1
+            either = here0 | here1
+            for m in range(16):
+                block = mat[m]
+                gfull[it, 8 * m : 8 * m + 8, :] = (
+                    jnp.where(either, 0.0, block)
+                    - spread(block, at0) * new0
+                    - spread(block, at0 + 1) * new1
+                )
+            gfull[it, pl.ds(k, 1), :] = new0[0:1]
+            gfull[it, pl.ds(k + 1, 1), :] = new1[0:1]
             return carry
 
         def invert(low, high):
@@ -651,12 +676,12 @@
             ring_second(0)
             ring_second(1)
             await_bytes(gfull.at[it, pl.ds(0, 16 * (NZ - 1))], rsem.at[it, number("gd")])
-            invert(0, 8)
+            invert(0, 10)
             ring_step(0, 1)
             ring_step(1, 1)
             fold_b(0, 1)
             fold_b(1, 3)
-            invert(8, 24)
+            invert(10, 26)
             ring_step(0, 2)
             ring_step(1, 2)
             arrive(("shi", 0), sibr_i.at[it, 0])
@@ -664,12 +689,12 @@
             half_a()
             take_b(1)
             take_b(3)
-            invert(24, 40)
+            invert(26, 42)
             ring_step(0, 3)
             ring_step(1, 3)
             fold_a()
             take_b(0)
-            invert(40, TILE)
+            invert(42, TILE // 2)
             finish(after_users, after_items)
 
         def finish(after_users, after_items):
@@ -718,7 +743,7 @@
             await_bytes(gfull.at[it, pl.ds(0, 16 * (NZ - 1))], ssem.at[it, number("gd")])
             assert len(names) <= 128, len(names)
 
-        return start_users, start_items, gather, gram_whole, terms, reduce, drain
+        return start_users, start_items, gather, terms, reduce, drain
 
     def send_lists():
         for d in range(1, NZ):
@@ -743,9 +768,8 @@
     phases[0][1]()
     send_lists()
     for it in range(ITERS):
-        _, _, gather, gram_whole, terms, reduce, drain = phases[it]
+        _, _, gather, terms, reduce, drain = phases[it]
         gather()
-        gram_whole()
         terms()
         if it + 1 < ITERS:
             reduce(phases[it + 1][0], phases[it + 1][1])

time: 129 us -> 117 us (0.907)
  Pallas kernels: 126 us -> 114 us
    pallas_call x1, Pallas kernels: 124 us -> 112 us  [on_device(): pl.pallas_call(functools.partial(kernel, user_coef, item_coef), out_shape...]
where the time goes in v3:
time: 117 us
  Pallas kernels  114 us (97%)
  local copies, waits for them, and re-layouts  1.51 us (1%)
    pallas_call x1, Pallas kernels, on_device(): pl.pallas_call(functools.partial(kernel, user_coef, item_coef), out_shape...  112 us

profile of v3, /device:TPU:1, one launch (start us, length us, event | category | flops | bytes accessed | tf_op | source)
XLA Modules:
  0.0 116.7 jit_solution(1597555913350647027)
XLA Ops:
  0.6 0.8 copy.11
  1.4 0.8 copy.12
  2.1 0.6 pad_add_fusion.sends
  2.7 112.0 %scaled_gd.1 = (f32[8,128,128]{2,1,0:T(8,128)}, f32[4,128,128]{2,1,0:T(8,128)}) custom-call(s32[1,64]{1,0:T(1,128)} %bitcast.18, s32[1,64]{1,0:T(1,128)} %bitcast.19, s32[24,128]{1,0:T(8,128)} %pad_add_fusion.sends, s32[64,128]{1,0:T(8,128)} %bitcast.14, s32[64,128]{1,0:T(8,128)} %bitcast.15, f32[8,128,128]{2,1,0:T(8,128)} %bitcast.12, ...), custom_call_target="tpu_custom_call" | custom-call | tf_op jit(solution)/shard_map/scaled_gd/pallas_call | solution.py:818
  114.7 2.0 %write_out.1 = (f32[8,128,128]{2,1,0:T(8,128)}, f32[4,128,128]{2,1,0:T(8,128)}) custom-call(f32[8,128,128]{2,1,0:T(8,128)} %get-tuple-element.6.new_u, f32[4,128,128]{2,1,0:T(8,128)} %get-tuple-element.7.new_i), custom_call_target="tpu_custom_call" | custom-call | tf_op jit(solution)/shard_map/write_out/pallas_call | solution.py:891

commit v4 on v3

--- a/solution.py
+++ b/solution.py
@@ -16,6 +16,7 @@
 LT = 8
 RT = 4
 NT = 64
+PIVOTS = 4
 CAPL = 4
 CAPR = 2
 HU = LT // 2
@@ -30,7 +31,8 @@
     item_coef,
     row_slots,
     col_slots,
-    sends,
+    send_users,
+    send_items,
     row_mask,
     col_mask,
     users,
@@ -38,6 +40,7 @@
     ratings,
     out_u,
     out_i,
+    sends,
     lists_u,
     lists_i,
     rows_u,
@@ -117,6 +120,10 @@
 
     sibling = {"rep": other}
 
+    sends[...] = jnp.zeros((8, TILE), jnp.int32)
+    sends[0:CAPL, 0:NZ] = send_users[...]
+    sends[CAPL : CAPL + CAPR, 0:NXY] = send_items[...]
+
     load_r = pltpu.make_async_copy(ratings, rat, lsem.at[0])
     load_u = pltpu.make_async_copy(users.at[pl.ds(HU * c, HU)], u_cur, lsem.at[1])
     load_i = pltpu.make_async_copy(items.at[pl.ds(HI * c, HI)], i_cur, lsem.at[2])
@@ -207,12 +214,17 @@
         await_bytes(lists_u.at[pl.ds(0, NZ - 1)], lsem.at[4])
         await_bytes(lists_i.at[pl.ds(0, NXY - 1)], lsem.at[5])
         await_bytes(lists_i.at[pl.ds(0, NXY - 1)], lsem.at[6])
-        rows_u[...] = jnp.concatenate(
-            [lists_u[s, pl.ds(z, 1), :] for s in range(NZ)], axis=0
-        )
-        rows_i[...] = jnp.concatenate(
-            [lists_i[s, pl.ds(trow, 1), :] for s in range(NXY)], axis=0
-        )
+        def spread(value, at):
+            return jnp.sum(jnp.where(lane8 == at, value.astype(F32), 0.0), axis=1, keepdims=True)
+
+        gathered_u = jnp.zeros((8, TILE), F32)
+        for s in range(NZ):
+            gathered_u = jnp.where(lane8 == s, spread(lists_u[s], z), gathered_u)
+        rows_u[...] = jnp.minimum(jnp.maximum(gathered_u.astype(jnp.int32), 0), LT - 1)
+        gathered_i = jnp.zeros((8, TILE), F32)
+        for s in range(NXY):
+            gathered_i = jnp.where(lane8 == s, spread(lists_i[s], trow), gathered_i)
+        rows_i[...] = jnp.minimum(jnp.maximum(gathered_i.astype(jnp.int32), 0), RT - 1)
         down_u = pltpu.make_async_copy(rows_u, slists_u, lsem.at[7])
         down_i = pltpu.make_async_copy(rows_i, slists_i, lsem.at[8])
         down_u.start()
@@ -225,11 +237,13 @@
 
         def user_tile(slot):
             source = slot // CAPL
-            return source * LT + slists_u[source, slot % CAPL]
+            tile = source * LT + slists_u[slot % CAPL, source]
+            return jnp.minimum(jnp.maximum(tile, 0), NT - 1)
 
         def item_tile(slot):
             source = slot // CAPR
-            return source * RT + slists_i[source, slot % CAPR]
+            tile = source * RT + slists_i[CAPL + slot % CAPR, source]
+            return jnp.minimum(jnp.maximum(tile, 0), NT - 1)
 
         def one(k, carry):
             x_row[k] = user_tile(tab[1, k])
@@ -239,14 +253,14 @@
             found = jnp.int32(NT)
             for s in range(CAPL):
                 found = jnp.where(
-                    slists_u[source, s] == k % LT, tab[6, source * CAPL + s], found
+                    slists_u[s, source] == k % LT, tab[6, source * CAPL + s], found
                 )
             tab_u[k] = found
             source = k // RT
             found = jnp.int32(NT)
             for s in range(CAPR):
                 found = jnp.where(
-                    slists_i[source, s] == k % RT,
+                    slists_i[CAPL + s, source] == k % RT,
                     tab[7, source * CAPR + s],
                     found,
                 )
@@ -591,37 +605,46 @@
                 begin(("h", w), half_s.at[w], half_r.at[it, w], {"trow": cell(0, ob)})
 
         def eliminate(n, carry):
-            k = 2 * n
+            k = PIVOTS * n
             mat = gfull[it].reshape(16, 8, TILE)
-            row0 = jnp.broadcast_to(gfull[it, pl.ds(k, 1), :], (8, TILE))
-            row1 = jnp.broadcast_to(gfull[it, pl.ds(k + 1, 1), :], (8, TILE))
-            at0 = jnp.full((8, TILE), k, jnp.int32)
-
-            def spread(value, at):
-                return jnp.take_along_axis(value, at, axis=1, mode="promise_in_bounds")
-
-            p = spread(row0, at0)
-            q = spread(row0, at0 + 1)
-            r = spread(row1, at0 + 1)
-            inv_p = 1.0 / p
-            t = q * inv_p
-            inv_s = 1.0 / (r - q * t)
-            here0 = lane8 == k
-            here1 = lane8 == k + 1
-            row0 = jnp.where(here0, 1.0, jnp.where(here1, 0.0, row0))
-            row1 = jnp.where(here1, 1.0, jnp.where(here0, 0.0, row1))
-            new1 = (row1 - t * row0) * inv_s
-            new0 = row0 * inv_p - t * new1
-            either = here0 | here1
+            at = [jnp.full((8, TILE), k + j, jnp.int32) for j in range(PIVOTS)]
+
+            def spread(value, j):
+                return jnp.take_along_axis(value, at[j], axis=1, mode="promise_in_bounds")
+
+            rows = [
+                jnp.broadcast_to(gfull[it, pl.ds(k + i, 1), :], (8, TILE)) for i in range(PIVOTS)
+            ]
+            core = [
+                [spread(rows[i], j) if j >= i else None for j in range(PIVOTS)]
+                for i in range(PIVOTS)
+            ]
+            for i in range(PIVOTS):
+                for j in range(i):
+                    core[i][j] = core[j][i]
+            inside = (lane8 >= k) & (lane8 < k + PIVOTS)
+            rows = [
+                jnp.where(lane8 == k + i, 1.0, jnp.where(inside, 0.0, rows[i]))
+                for i in range(PIVOTS)
+            ]
+            for i in range(PIVOTS):
+                scale = 1.0 / core[i][i]
+                rows[i] = rows[i] * scale
+                for j in range(i + 1, PIVOTS):
+                    core[i][j] = core[i][j] * scale
+                for m in range(PIVOTS):
+                    if m != i:
+                        for j in range(i + 1, PIVOTS):
+                            core[m][j] = core[m][j] - core[m][i] * core[i][j]
+                        rows[m] = rows[m] - core[m][i] * rows[i]
             for m in range(16):
                 block = mat[m]
-                gfull[it, 8 * m : 8 * m + 8, :] = (
-                    jnp.where(either, 0.0, block)
-                    - spread(block, at0) * new0
-                    - spread(block, at0 + 1) * new1
-                )
-            gfull[it, pl.ds(k, 1), :] = new0[0:1]
-            gfull[it, pl.ds(k + 1, 1), :] = new1[0:1]
+                value = jnp.where(inside, 0.0, block)
+                for j in range(PIVOTS):
+                    value = value - spread(block, j) * rows[j]
+                gfull[it, 8 * m : 8 * m + 8, :] = value
+            for i in range(PIVOTS):
+                gfull[it, pl.ds(k + i, 1), :] = rows[i][0:1]
             return carry
 
         def invert(low, high):
@@ -655,7 +678,7 @@
 
         def half_a():
             for w, oa in ((0, 1), (1, 3)):
-                ah_s[w] = quarter[2, w].astype(BF16)
+                ah_s[w] = quarter[2, w]
                 begin(("ah", w), ah_s.at[w], ah_r.at[it, w], {"trow": cell(oa, 0)})
 
         def fold_a():
@@ -664,8 +687,8 @@
                 for j in range(HI):
                     value = quarter[oa, j]
                     if j == w:
-                        value = value + ah_r[it, w].astype(F32)
-                    af_s[w, j] = value.astype(BF16)
+                        value = value + ah_r[it, w]
+                    af_s[w, j] = value
                 begin(("af2", w), af_s.at[w], af_r.at[it, w], {"trow": cell(oa, 0)})
 
         def reduce(after_users, after_items):
@@ -676,12 +699,12 @@
             ring_second(0)
             ring_second(1)
             await_bytes(gfull.at[it, pl.ds(0, 16 * (NZ - 1))], rsem.at[it, number("gd")])
-            invert(0, 10)
+            invert(0, 5)
             ring_step(0, 1)
             ring_step(1, 1)
             fold_b(0, 1)
             fold_b(1, 3)
-            invert(10, 26)
+            invert(5, 13)
             ring_step(0, 2)
             ring_step(1, 2)
             arrive(("shi", 0), sibr_i.at[it, 0])
@@ -689,12 +712,12 @@
             half_a()
             take_b(1)
             take_b(3)
-            invert(26, 42)
+            invert(13, 21)
             ring_step(0, 3)
             ring_step(1, 3)
             fold_a()
             take_b(0)
-            invert(42, TILE // 2)
+            invert(21, TILE // PIVOTS)
             finish(after_users, after_items)
 
         def finish(after_users, after_items):
@@ -722,7 +745,7 @@
                 arrive(("af2", w), af_r.at[it, w])
             grad_i = jnp.concatenate(
                 [
-                    quarter[0, j] + af_r[it, 0, j].astype(F32) + af_r[it, 1, j].astype(F32)
+                    quarter[0, j] + af_r[it, 0, j] + af_r[it, 1, j]
                     for j in range(HI)
                 ],
                 axis=0,
@@ -748,18 +771,18 @@
     def send_lists():
         for d in range(1, NZ):
             remote(
-                sends.at[pl.ds(0, NZ)], lists_u.at[z], lsem.at[3], lsem.at[4], {"tcol": (z + d) % NZ}
+                sends, lists_u.at[z], lsem.at[3], lsem.at[4], {"tcol": (z + d) % NZ}
             ).start()
         for d in range(1, NXY):
             remote(
-                sends.at[pl.ds(NZ, NXY)],
+                sends,
                 lists_i.at[trow],
                 lsem.at[5],
                 lsem.at[6],
                 {"trow": (trow + d) % NXY},
             ).start()
-        lists_u[z] = sends[0:NZ, :]
-        lists_i[trow] = sends[NZ : NZ + NXY, :]
+        lists_u[z] = sends[...]
+        lists_i[trow] = sends[...]
 
     last_u = remote(u_cur, out_u.at[pl.ds(HU * c, HU)], lsem.at[1], lsem.at[7], sibling)
     last_i = remote(i_cur, out_i.at[pl.ds(HI * c, HI)], lsem.at[2], lsem.at[8], sibling)
@@ -803,14 +826,6 @@
     all_items = own_items * TILE * NXY * NZ
     user_coef = 2.0 * all_items * own_users / (TILE * NT * 2)
     item_coef = 2.0 * all_users * own_items / (TILE * NT * 2)
-    sends = jnp.concatenate(
-        [
-            jnp.pad(send_users.reshape(NZ, CAPL), ((0, 0), (0, TILE - CAPL))),
-            jnp.pad(send_items.reshape(NXY, CAPR), ((0, 0), (0, TILE - CAPR))),
-        ],
-        axis=0,
-    )
-
     any_spec = pl.BlockSpec(memory_space=pl.ANY)
     vmem_spec = pl.BlockSpec(memory_space=pltpu.VMEM)
     square = (TILE, TILE)
@@ -821,15 +836,16 @@
             jax.ShapeDtypeStruct((LT,) + square, F32),
             jax.ShapeDtypeStruct((RT,) + square, F32),
         ),
-        in_specs=[vmem_spec] * 5 + [any_spec] * 3,
+        in_specs=[vmem_spec] * 6 + [any_spec] * 3,
         out_specs=(vmem_spec, vmem_spec),
         scratch_shapes=[
-            pltpu.VMEM((NZ, NZ, TILE), jnp.int32),
-            pltpu.VMEM((NXY, NXY, TILE), jnp.int32),
-            pltpu.VMEM((NZ, TILE), jnp.int32),
-            pltpu.VMEM((NXY, TILE), jnp.int32),
-            pltpu.SMEM((NZ, TILE), jnp.int32),
-            pltpu.SMEM((NXY, TILE), jnp.int32),
+            pltpu.VMEM((8, TILE), jnp.int32),
+            pltpu.VMEM((NZ, 8, TILE), jnp.int32),
+            pltpu.VMEM((NXY, 8, TILE), jnp.int32),
+            pltpu.VMEM((8, TILE), jnp.int32),
+            pltpu.VMEM((8, TILE), jnp.int32),
+            pltpu.SMEM((8, TILE), jnp.int32),
+            pltpu.SMEM((8, TILE), jnp.int32),
             pltpu.VMEM((8, TILE), jnp.int32),
             pltpu.SMEM((8, TILE), jnp.int32),
             table,
@@ -866,10 +882,10 @@
             pltpu.VMEM((2, 4, HI) + square, BF16),
             pltpu.VMEM((ITERS, 2, 4, HI) + square, BF16),
             pltpu.VMEM((4, HI) + square, F32),
-            pltpu.VMEM((2,) + square, BF16),
-            pltpu.VMEM((ITERS, 2) + square, BF16),
-            pltpu.VMEM((2, HI) + square, BF16),
-            pltpu.VMEM((ITERS, 2, HI) + square, BF16),
+            pltpu.VMEM((2,) + square, F32),
+            pltpu.VMEM((ITERS, 2) + square, F32),
+            pltpu.VMEM((2, HI) + square, F32),
+            pltpu.VMEM((ITERS, 2, HI) + square, F32),
             pltpu.SemaphoreType.DMA((ITERS, 128)),
             pltpu.SemaphoreType.DMA((ITERS, 128)),
             pltpu.SemaphoreType.DMA((10,)),
@@ -881,7 +897,8 @@
     )(
         row_slots.reshape(1, NT),
         col_slots.reshape(1, NT),
-        sends,
+        send_users.reshape(NZ, CAPL).T,
+        send_items.reshape(NXY, CAPR).T,
         row_mask.reshape(NT, TILE),
         col_mask.reshape(NT, TILE),
         users.reshape((LT,) + square),

time: 117 us -> 115 us (0.983)
  local copies, waits for them, and re-layouts: 1.51 us -> 0 us
    reshape x2 -> x0, local copies, waits for them, and re-layouts: 1.51 us -> none  [the longest x1 0.76 us: on_device(): send_users.reshape(NZ, CAPL)]
where the time goes in v4:
time: 115 us
  Pallas kernels  115 us (100%)
    pallas_call x1, Pallas kernels, on_device(): pl.pallas_call(functools.partial(kernel, user_coef, item_coef), out_shape...  113 us

profile of v4, /device:TPU:1, one launch (start us, length us, event | category | flops | bytes accessed | tf_op | source)
XLA Modules:
  0.0 115.3 jit_solution(15956947871270871882)
XLA Ops:
  0.6 112.6 %scaled_gd.1 = (f32[8,128,128]{2,1,0:T(8,128)}, f32[4,128,128]{2,1,0:T(8,128)}) custom-call(s32[1,64]{1,0:T(1,128)} %bitcast.22, s32[1,64]{1,0:T(1,128)} %bitcast.23, s32[4,8]{1,0:T(4,128)} %bitcast.20, s32[2,16]{1,0:T(2,128)} %bitcast.21, s32[64,128]{1,0:T(8,128)} %bitcast.18, s32[64,128]{1,0:T(8,128)} %bitcast.19, f32[8,128,128]{2,1,0:T(8,128)} %bitcast.16, ...), custom_call_target="tpu_custom_call" | custom-call | tf_op jit(solution)/shard_map/scaled_gd/pallas_call | solution.py:833
  113.3 2.0 %write_out.1 = (f32[8,128,128]{2,1,0:T(8,128)}, f32[4,128,128]{2,1,0:T(8,128)}) custom-call(f32[8,128,128]{2,1,0:T(8,128)} %get-tuple-element.6.new_u, f32[4,128,128]{2,1,0:T(8,128)} %get-tuple-element.7.new_i), custom_call_target="tpu_custom_call" | custom-call | tf_op jit(solution)/shard_map/write_out/pallas_call | solution.py:908
